TPU v7x, 128 devices: a whole 4x4x4 slice. The times are simulated.
128 devices in a mesh: node: 32 (over y_hi, z, x), query: 4 (over y_lo, core).
Axes of the slice: x: 4, y: 4 (y_hi: 2, y_lo: 2; y = y_hi * 2 + y_lo), z: 4, core: 2. Of those that a mesh axis runs over, the one named last changes fastest.
Arguments:
- entity_state: bfloat16 [32768, 2048], P('node', 'query'), may hold values from -6 to 6
- edge_tiles: int32 [512, 3, 512], P('node'), may hold values from 0 to 4095, as said below
- query_head: int32 [64], P('query'), may hold values from 0 to 32767
- query_relation: int32 [64], P('query'), may hold values from 0 to 821
- query_table: float32 [822, 32], replicated, may hold values from -6 to 6
- rel_vectors: float32 [2, 822, 32], replicated, may hold values from -1.8 to 1.8
- mix_weight: float32 [2, 32, 32], replicated, may hold values from -1 to 1
- mix_bias: float32 [2, 32], replicated, may hold values from -3 to 3
- cotangent: bfloat16 [32768, 2048], P('node', 'query'), may hold values from -6 to 6
Outputs:
- final_state: bfloat16 [32768, 2048], P('node', 'query')
- weight_grads: float32 [2, 32, 32], replicated
- bias_grads: float32 [2, 32], replicated
Inputs may be any that keep to these rules, and one draw needn't show every extreme that they name: edge_tiles[t,0,:] lies in 0 to 4095, edge_tiles[t,1,:] in 0 to 63, edge_tiles[t,2,:] in 0 to 821.
All inputs are finite; a program needn't handle non-finite values.
Results may differ from a plain program's by a relative error of at most 0.0056.
Values may be sent and summed in bfloat16 or wider, within the bound.
A program may use at most 192 MiB of HBM per device.

v0:
```python
import jax
import jax.numpy as jnp
from jax import lax
from jax.sharding import PartitionSpec as P

DIM = 32


def with_halo(block, sides, width):
    for axis, dim in sides:
        count = lax.axis_size(axis)
        forward = [(i, i + 1) for i in range(count - 1)]
        forward.append((count - 1, 0))
        backward = [(target, source) for source, target in forward]
        low = lax.ppermute(
            lax.slice_in_dim(block, block.shape[dim] - width, None, axis=dim), axis, forward
        )
        high = lax.ppermute(lax.slice_in_dim(block, 0, width, axis=dim), axis, backward)
        block = jnp.concatenate([low, block, high], axis=dim)
    return block


def from_partner(block, axis, apart):
    count = lax.axis_size(axis)
    route = []
    for low in range(count):
        high = low | 1 << apart
        if high != low and high < count:
            route += [(low, high), (high, low)]
    return lax.ppermute(block, axis, route)


def passed_along(block, axis, distance):
    devices = range(lax.axis_size(axis))
    route = [((i - distance) % len(devices), i) for i in devices]
    return lax.ppermute(block, axis, route)


def silu_slope(values):
    sigma = jax.nn.sigmoid(values)
    return sigma * (1.0 + values * (1.0 - sigma))


def target_onehot(edge_block):
    return (edge_block[:, 1, :][:, None, :] == lax.iota(jnp.int32, 64)[None, :, None]).astype(
        jnp.bfloat16
    )


def contributions(grad_panel, edge_block, dst_onehot, rel_table, slot_base, slot_count):
    tile_count = edge_block.shape[0]
    slot_total = edge_block.shape[2]
    col_count = grad_panel.shape[1]
    per_edge = jnp.einsum(
        "tre,trc->tec",
        dst_onehot,
        grad_panel.reshape(tile_count, 64, col_count),
        preferred_element_type=jnp.float32,
    )
    rel_scales = jnp.take(rel_table, edge_block[:, 2, :], axis=0)
    edge_terms = (
        per_edge.reshape(tile_count, slot_total, col_count // DIM, DIM) * rel_scales[:, :, None, :]
    ).reshape(tile_count * slot_total, col_count)
    segment_ids = edge_block[:, 0, :].reshape(-1) - slot_base
    segment_ids = jnp.where(
        (segment_ids >= 0) & (segment_ids < slot_count), segment_ids, slot_count
    )
    summed = jax.ops.segment_sum(edge_terms, segment_ids, num_segments=slot_count + 1)
    return summed[:slot_count]


def reduce_grads(values):
    return lax.psum((values[0], values[1]), ("node", "query"))


def body(
    entity_state,
    edge_tiles,
    query_head,
    query_relation,
    query_table,
    rel_vectors,
    mix_weight,
    mix_bias,
    cotangent,
):
    highest = lax.Precision.HIGHEST
    row_count = entity_state.shape[0]
    tile_count = edge_tiles.shape[0]
    slot_total = edge_tiles.shape[2]
    query_count = query_head.shape[0]
    col_count = query_count * DIM
    mirror_bit = lax.axis_size("node").bit_length() - 2
    first_row = lax.axis_index("node") * row_count
    entity_ids = first_row + lax.iota(jnp.int32, row_count)
    choose_rel = (
        query_relation[:, None] == lax.iota(jnp.int32, query_table.shape[0])[None, :]
    ).astype(jnp.float32)
    query_vec = jnp.dot(
        choose_rel, query_table, precision=highest, preferred_element_type=jnp.float32
    )
    head_match = (entity_ids[:, None] == query_head[None, :]).astype(jnp.float32)
    boundary = (
        (head_match[:, :, None] * query_vec[None, :, :])
        .reshape(row_count, col_count)
        .astype(jnp.bfloat16)
    )
    own_onehot = target_onehot(edge_tiles)

    def window(state_panel):
        sides = with_halo(state_panel, (("node", 0),), row_count)
        mirror = from_partner(state_panel, "node", mirror_bit)
        return jnp.concatenate([sides, mirror], axis=0)

    def run_layer(state_panel, layer_index):
        extended = window(state_panel)
        gathered = jnp.take(extended, edge_tiles[:, 0, :], axis=0)
        rel_scales = jnp.take(rel_vectors[layer_index], edge_tiles[:, 2, :], axis=0)
        message = (
            gathered.reshape(tile_count, slot_total, query_count, DIM) * rel_scales[:, :, None, :]
        ).astype(jnp.bfloat16)
        message = message.reshape(tile_count, slot_total, col_count)
        summed = jnp.einsum(
            "tre,tec->trc", own_onehot, message, preferred_element_type=jnp.float32
        ).reshape(row_count, col_count)
        mixed_in = boundary.astype(jnp.float32) + summed
        update = (
            jnp.einsum(
                "rqd,de->rqe",
                mixed_in.reshape(row_count, query_count, DIM),
                mix_weight[layer_index],
                precision=highest,
            )
            + mix_bias[layer_index]
        )
        result = (
            state_panel.astype(jnp.float32) + jax.nn.silu(update).reshape(row_count, col_count)
        ).astype(jnp.bfloat16)
        return (mixed_in, update, result)

    mixed_zero, update_zero, state_one = run_layer(entity_state, 0)
    mixed_one, update_one, state_two = run_layer(state_one, 1)
    grad_out = cotangent.astype(jnp.float32)
    grad_update_one = grad_out.reshape(row_count, query_count, DIM) * silu_slope(update_one)
    weight_one = jnp.einsum(
        "rqd,rqe->de",
        mixed_one.reshape(row_count, query_count, DIM),
        grad_update_one,
        precision=highest,
    )
    bias_one = jnp.sum(grad_update_one, axis=(0, 1))
    weight_one, bias_one = reduce_grads((weight_one, bias_one))
    grad_mixed_one = (
        jnp.einsum("rqe,de->rqd", grad_update_one, mix_weight[1], precision=highest)
        .reshape(row_count, col_count)
        .astype(jnp.bfloat16)
    )
    window_terms = contributions(
        grad_mixed_one, edge_tiles, own_onehot, rel_vectors[1], 0, 4 * row_count
    )
    own_terms = window_terms[row_count : 2 * row_count]
    back_right = passed_along(window_terms[:row_count].astype(jnp.bfloat16), "node", -1)
    back_left = passed_along(
        window_terms[2 * row_count : 3 * row_count].astype(jnp.bfloat16), "node", 1
    )
    back_mirror = from_partner(
        window_terms[3 * row_count :].astype(jnp.bfloat16), "node", mirror_bit
    )
    adjoint_sum = (
        own_terms
        + back_right.astype(jnp.float32)
        + back_left.astype(jnp.float32)
        + back_mirror.astype(jnp.float32)
    )
    grad_state_one = grad_out + adjoint_sum
    grad_update_zero = grad_state_one.reshape(row_count, query_count, DIM) * silu_slope(update_zero)
    weight_zero = jnp.einsum(
        "rqd,rqe->de",
        mixed_zero.reshape(row_count, query_count, DIM),
        grad_update_zero,
        precision=highest,
    )
    bias_zero = jnp.sum(grad_update_zero, axis=(0, 1))
    weight_zero, bias_zero = reduce_grads((weight_zero, bias_zero))
    weight_grads = jnp.stack([weight_zero, weight_one])
    bias_grads = jnp.stack([bias_zero, bias_one])
    return (state_two, weight_grads, bias_grads)


def solution(mesh):
    placed = (
        P("node", "query"),
        P("node", None, None),
        P("query"),
        P("query"),
        P(),
        P(),
        P(),
        P(),
        P("node", "query"),
    )
    return jax.shard_map(
        body, mesh=mesh, in_specs=placed, out_specs=(P("node", "query"), P(), P()), check_vma=False
    )
```

profile of v0, /device:TPU:0, one launch (start us, length us, event | category | flops | bytes accessed | tf_op | source)
XLA Modules:
  0.0 584.1 jit_solution(341249885668741540)
XLA Ops:
  0.6 9.0 %collective-permute-start.1 = (bf16[1024,512]{1,0:T(8,128)(2,1)}, bf16[1024,512]{1,0:T(8,128)(2,1)}, u32[]{:S(2)}, u32[]{:S(2)}) collective-permute-start(bf16[1024,512]{1,0:T(8,128)(2,1)} %param.13), channel_id=1, source_target_pairs={{4,0},{8,4},{12,8},{16,12},{20,16},{24,20},{28,24},{32,28},{36,32}... | collective-permute-start | bytes 3145736 | tf_op jit(solution)/shard_map/ppermute | solution.py:18
  13.0 27.8 %gather_fusion.1 = f32[8192,32]{1,0:T(8,128)} fusion(f32[822,32]{1,0:T(8,128)S(1)} %bitcast.102, s32[8192]{0:T(1024)S(1)} %broadcast_clamp_fusion), kind=kCustom, calls=%fused_computation.1.clone | custom fusion | bytes 2129920 | tf_op jit(solution)/shard_map/jit(_take)/gather | solution.py:118
  40.7 27.7 %gather_fusion.3 = f32[8192,32]{1,0:T(8,128)} fusion(f32[822,32]{1,0:T(8,128)S(1)} %bitcast.101, s32[8192]{0:T(1024)S(1)} %broadcast_clamp_fusion), kind=kCustom, calls=%fused_computation.3.clone | custom fusion | bytes 2129920 | tf_op jit(solution)/shard_map/jit(_take)/gather | solution.py:118
  68.5 7.5 %broadcast_select_fusion = (f32[16,512,32]{2,1,0:T(8,128)}, f32[16,512,32]{2,1,0:T(8,128)}) fusion(f32[16,512,32]{2,1,0:T(8,128)} %bitcast.109, pred[16,512]{1,0:T(8,128)(4,1)S(1)} %get-tuple-element.22, f32[16,512,32]{2,1,0:T(8,128)} %bitcast.108), kind=kLoop, calls=%fused_computation.25 | loop fusion | flops 524288 | bytes 4202496 | tf_op jit(solution)/shard_map/jit(_take)/select_n | solution.py:118
  99.1 17.7 %copy.64 = f32[64,8,16,512]{3,1,2,0:T(8,128)} copy(f32[64,8,16,512]{3,2,1,0:T(8,128)S(1)} %bitcast.105) | data formatting | bytes 33554432
  120.4 36.5 %gather_fusion = bf16[8192,512]{1,0:T(8,128)(2,1)} fusion(bf16[4096,512]{1,0:T(8,128)(2,1)} %pad_maximum_fusion, s32[8192]{0:T(1024)S(1)} %broadcast_clamp_fusion.1), kind=kCustom, calls=%fused_computation.clone | custom fusion | bytes 16809984 | tf_op jit(solution)/shard_map/jit(_take)/gather | solution.py:117
  156.9 12.4 %copy.28 = bf16[16,512,512]{1,2,0:T(8,128)(2,1)} copy(bf16[16,512,512]{2,1,0:T(8,128)(2,1)} %bitcast.107) | data formatting | bytes 16777216 | tf_op jit(solution)/shard_map/jit(_take)/gather | solution.py:117
  169.4 9.7 %fusion.1 = bf16[16,512,512]{1,2,0:T(8,128)(2,1)} fusion(bf16[16,512,512]{1,2,0:T(8,128)(2,1)} %copy.28, f32[16,512,32]{1,2,0:T(8,128)} %copy.30, pred[16,512]{1,0:T(8,128)(4,1)S(1)} %get-tuple-element.21), kind=kLoop, calls=%fused_computation.8 | loop fusion | flops 16777216 | bytes 17833984 | tf_op jit(solution)/shard_map/convert_element_type | solution.py:121
  179.0 8.0 %convert_add_fusion.3 = (f32[16,64,512]{2,1,0:T(8,128)}, f32[16,64,512]{2,1,0:T(8,128)}) fusion(f32[16,64,512]{2,1,0:T(8,128)S(1)} %copy.27, f32[512]{0:T(512)S(1)} %mul.88, bf16[16,512,512]{1,2,0:T(8,128)(2,1)} %fusion.1, s32[16,512]{1,0:T(8,128)S(1)} %get-tuple-element.20), kind=kOutput, calls=%fused_computation.16 | convolution fusion | flops 539492352 | bytes 14714880 | tf_op jit(solution)/shard_map/tre,tec->trc/dot_general | solution.py:123
  187.1 4.8 copy.32
  191.9 4.9 add.106
  196.8 5.9 %fusion.12 = (f32[1024,16,32]{0,2,1:T(8,128)}, f32[1024,16,32]{0,2,1:T(8,128)}) fusion(f32[32]{0:T(128)S(1)} %get-tuple-element.28, f32[1024,16,32]{0,2,1:T(8,128)} %add.106, f32[2,32,32]{2,1,0:T(8,128)S(1)} %copy-done.15), kind=kOutput, calls=%fused_computation.35 | convolution fusion | flops 203948032 | bytes 6308352 | tf_op jit(solution)/shard_map/rqd,de->rqe/dot_general | solution.py:128
  211.0 7.7 %collective-permute-start.4 = (bf16[1024,512]{1,0:T(8,128)(2,1)S(1)}, bf16[1024,512]{1,0:T(8,128)(2,1)S(1)}, u32[]{:S(2)}, u32[]{:S(2)}) collective-permute-start(bf16[1024,512]{1,0:T(8,128)(2,1)S(1)} %add_convert_fusion.1), channel_id=1, source_target_pairs={{4,0},{8,4},{12,8},{16,12},{20,16},{24,20},{28,24},{32,28},{36,32}... | collective-permute-start | bytes 3145736 | tf_op jit(solution)/shard_map/ppermute | solution.py:18
  218.8 14.9 %collective-permute-done.5 = bf16[1024,512]{1,0:T(8,128)(2,1)S(1)} collective-permute-done((bf16[1024,512]{1,0:T(8,128)(2,1)S(1)}, bf16[1024,512]{1,0:T(8,128)(2,1)S(1)}, u32[]{:S(2)}, u32[]{:S(2)}) %collective-permute-start.5) | collective-permute-done | bytes 1048608 | tf_op jit(solution)/shard_map/ppermute | solution.py:30
  233.7 6.4 %collective-permute-done.4 = bf16[1024,512]{1,0:T(8,128)(2,1)S(1)} collective-permute-done((bf16[1024,512]{1,0:T(8,128)(2,1)S(1)}, bf16[1024,512]{1,0:T(8,128)(2,1)S(1)}, u32[]{:S(2)}, u32[]{:S(2)}) %collective-permute-start.4) | collective-permute-done | bytes 1048608 | tf_op jit(solution)/shard_map/ppermute | solution.py:18
  240.1 8.0 %collective-permute-done.3 = bf16[1024,512]{1,0:T(8,128)(2,1)S(1)} collective-permute-done((bf16[1024,512]{1,0:T(8,128)(2,1)S(1)}, bf16[1024,512]{1,0:T(8,128)(2,1)S(1)}, u32[]{:S(2)}, u32[]{:S(2)}) %collective-permute-start.3) | collective-permute-done | bytes 1048608 | tf_op jit(solution)/shard_map/ppermute | solution.py:15
  250.5 36.5 %gather_fusion.2 = bf16[8192,512]{1,0:T(8,128)(2,1)} fusion(bf16[4096,512]{1,0:T(8,128)(2,1)} %pad_maximum_fusion.1, s32[8192]{0:T(1024)S(1)} %broadcast_clamp_fusion.1), kind=kCustom, calls=%fused_computation.2.clone | custom fusion | bytes 16809984 | tf_op jit(solution)/shard_map/jit(_take)/gather | solution.py:117
  287.0 12.3 %copy.35 = bf16[16,512,512]{1,2,0:T(8,128)(2,1)} copy(bf16[16,512,512]{2,1,0:T(8,128)(2,1)} %bitcast.106) | data formatting | bytes 16777216 | tf_op jit(solution)/shard_map/jit(_take)/gather | solution.py:117
  299.3 9.7 %fusion = bf16[16,512,512]{1,2,0:T(8,128)(2,1)} fusion(bf16[16,512,512]{1,2,0:T(8,128)(2,1)} %copy.35, f32[16,512,32]{1,2,0:T(8,128)} %copy.37, pred[16,512]{1,0:T(8,128)(4,1)S(1)} %get-tuple-element.21), kind=kLoop, calls=%fused_computation.6 | loop fusion | flops 16777216 | bytes 17833984 | tf_op jit(solution)/shard_map/convert_element_type | solution.py:121
  308.9 8.0 %convert_add_fusion.2 = (f32[16,64,512]{2,1,0:T(8,128)}, f32[16,64,512]{2,1,0:T(8,128)}) fusion(f32[16,64,512]{2,1,0:T(8,128)S(1)} %copy.27, f32[512]{0:T(512)S(1)} %mul.88, bf16[16,512,512]{1,2,0:T(8,128)(2,1)} %fusion, s32[16,512]{1,0:T(8,128)S(1)} %get-tuple-element.20), kind=kOutput, calls=%fused_computation.15 | convolution fusion | flops 539492352 | bytes 14714880 | tf_op jit(solution)/shard_map/tre,tec->trc/dot_general | solution.py:123
  317.0 4.8 copy.39
  325.3 5.8 fusion.37
  336.1 8.2 %fusion.9 = f32[16,512,512]{2,1,0:T(8,128)} fusion(bf16[16,64,512]{1,0,2:T(8,128)(2,1)S(1)} %convert_element_type.93, s32[16,512]{1,0:T(8,128)S(1)} %get-tuple-element.20), kind=kOutput, calls=%fused_computation.23 | convolution fusion | flops 537395200 | bytes 17858560 | tf_op jit(solution)/shard_map/tre,trc->tec/dot_general | solution.py:54
  344.3 17.4 %copy.47 = f32[8192,512]{0,1:T(8,128)} copy(f32[8192,512]{1,0:T(8,128)} %bitcast.104) | data formatting | bytes 33554432 | tf_op jit(solution)/shard_map/reshape | solution.py:62
  361.7 17.8 %mul.105 = f32[8192,512]{0,1:T(8,128)} multiply(f32[8192,512]{0,1:T(8,128)} %copy.47, f32[8192,512]{0,1:T(8,128)} %bitcast.103) | non-fusion elementwise | flops 4194304 | bytes 50331648 | tf_op jit(solution)/shard_map/mul | solution.py:62
  379.6 17.4 %copy.48 = f32[8192,512]{1,0:T(8,128)} copy(f32[8192,512]{0,1:T(8,128)} %mul.105) | data formatting | bytes 33554432 | tf_op jit(solution)/shard_map/mul | solution.py:62
  397.0 52.9 %scatter_custom_fusion = f32[4097,512]{1,0:T(8,128)} fusion(s32[8192]{0:T(1024)S(1)} %bitcast.117, f32[8192,512]{1,0:T(8,128)} %copy.48, f32[]{:T(128)} %constant.12.clone.1), kind=kCustom, calls=%fused_computation.9 | custom fusion | flops 4194304 | bytes 8391168 | tf_op jit(solution)/shard_map/scatter-add | solution.py:68
  449.9 3.9 convert.5
  468.4 4.8 copy.50
  473.2 5.0 reshape.154
  484.7 4.5 fusion.8
  497.3 85.4 %all-reduce = (f32[1,32,32]{2,1,0:T(8,128)S(1)}, f32[1,32,32]{2,1,0:T(8,128)S(1)}, f32[1,32]{1,0:T(1,128)S(1)}, f32[1,32]{1,0:T(1,128)S(1)}) all-reduce(f32[1,32,32]{2,1,0:T(8,128)S(1)} %fusion.15, f32[1,32,32]{2,1,0:T(8,128)S(1)} %fusion.16, f32[1,32]{1,0:T(1,128)S(1)} %bitcast.119, ...), channel_id=1, replica_groups=mesh['node'=32,'query'=4] {'node','query'}, use_global_device_ids=true, to_apply=%region_2.5 | all-reduce | flops 2112 | bytes 16896 | tf_op jit(solution)/shard_map/psum | solution.py:73
  (94 shorter events, 79.5 us)
Async XLA Ops:
  0.6 75.3 %copy-start = (f32[822,32]{0,1:T(8,128)S(1)}, f32[822,32]{0,1:T(8,128)}, u32[]{:S(2)}) copy-start(f32[822,32]{0,1:T(8,128)} %param.17) | copy-start | bytes 315652
  0.6 116.2 %collective-permute-start.1 = (bf16[1024,512]{1,0:T(8,128)(2,1)}, bf16[1024,512]{1,0:T(8,128)(2,1)}, u32[]{:S(2)}, u32[]{:S(2)}) collective-permute-start(bf16[1024,512]{1,0:T(8,128)(2,1)} %param.13), channel_id=1, source_target_pairs={{4,0},{8,4},{12,8},{16,12},{20,16},{24,20},{28,24},{32,28},{36,32}... | collective-permute-start | bytes 3145736 | tf_op jit(solution)/shard_map/ppermute | solution.py:18
  9.7 107.2 %collective-permute-start = (bf16[1024,512]{1,0:T(8,128)(2,1)}, bf16[1024,512]{1,0:T(8,128)(2,1)}, u32[]{:S(2)}, u32[]{:S(2)}) collective-permute-start(bf16[1024,512]{1,0:T(8,128)(2,1)} %param.13), channel_id=1, source_target_pairs={{0,4},{4,8},{8,12},{12,16},{16,20},{20,24},{24,28},{28,32},{32,36}... | collective-permute-start | bytes 3145736 | tf_op jit(solution)/shard_map/ppermute | solution.py:15
  9.7 107.2 %collective-permute-start.2 = (bf16[1024,512]{1,0:T(8,128)(2,1)}, bf16[1024,512]{1,0:T(8,128)(2,1)}, u32[]{:S(2)}, u32[]{:S(2)}) collective-permute-start(bf16[1024,512]{1,0:T(8,128)(2,1)} %param.13), channel_id=1, source_target_pairs={{0,64},{64,0},{4,68},{68,4},{8,72},{72,8},{12,76},{76,12},{16,80},... | collective-permute-start | bytes 3145736 | tf_op jit(solution)/shard_map/ppermute | solution.py:30
  68.5 7.5 %copy-start.17 = (s32[16]{0:T(128)S(1)}, s32[16]{0:T(128)}, u32[]{:S(2)}) copy-start(s32[16]{0:T(128)} %param.16) | copy-start | bytes 196
  76.2 7.4 %copy-start.13 = (f32[16,32]{1,0:T(8,128)}, f32[16,32]{1,0:T(8,128)S(1)}, u32[]{:S(2)}) copy-start(f32[16,32]{1,0:T(8,128)S(1)} %fusion.24) | copy-start | bytes 6148
  80.0 3.7 copy-start.12
  80.0 3.8 copy-start.18
  83.9 2.9 copy-start.10
  99.1 17.8 %copy-start.16 = (f32[2,32]{1,0:T(2,128)S(1)}, f32[2,32]{1,0:T(2,128)}, u32[]{:S(2)}) copy-start(f32[2,32]{1,0:T(2,128)} %param.20) | copy-start | bytes 772
  99.1 17.8 %copy-start.9 = (bf16[1024,512]{1,0:T(8,128)(2,1)S(1)}, bf16[1024,512]{1,0:T(8,128)(2,1)}, u32[]{:S(2)}) copy-start(bf16[1024,512]{1,0:T(8,128)(2,1)} %param.13) | copy-start | bytes 3145732
  191.9 4.9 copy-start.15
  207.7 40.4 %copy-start.2 = (bf16[1024,512]{1,0:T(8,128)(2,1)}, bf16[1024,512]{1,0:T(8,128)(2,1)S(1)}, u32[]{:S(2)}) copy-start(bf16[1024,512]{1,0:T(8,128)(2,1)S(1)} %add_convert_fusion.1) | copy-start | bytes 3145732
  207.7 25.9 %collective-permute-start.5 = (bf16[1024,512]{1,0:T(8,128)(2,1)S(1)}, bf16[1024,512]{1,0:T(8,128)(2,1)S(1)}, u32[]{:S(2)}, u32[]{:S(2)}) collective-permute-start(bf16[1024,512]{1,0:T(8,128)(2,1)S(1)} %add_convert_fusion.1), channel_id=1, source_target_pairs={{0,64},{64,0},{4,68},{68,4},{8,72},{72,8},{12,76},{76,12},{16,80},... | collective-permute-start | bytes 3145736 | tf_op jit(solution)/shard_map/ppermute | solution.py:30
  211.0 29.1 %collective-permute-start.4 = (bf16[1024,512]{1,0:T(8,128)(2,1)S(1)}, bf16[1024,512]{1,0:T(8,128)(2,1)S(1)}, u32[]{:S(2)}, u32[]{:S(2)}) collective-permute-start(bf16[1024,512]{1,0:T(8,128)(2,1)S(1)} %add_convert_fusion.1), channel_id=1, source_target_pairs={{4,0},{8,4},{12,8},{16,12},{20,16},{24,20},{28,24},{32,28},{36,32}... | collective-permute-start | bytes 3145736 | tf_op jit(solution)/shard_map/ppermute | solution.py:18
  218.8 29.3 %collective-permute-start.3 = (bf16[1024,512]{1,0:T(8,128)(2,1)S(1)}, bf16[1024,512]{1,0:T(8,128)(2,1)S(1)}, u32[]{:S(2)}, u32[]{:S(2)}) collective-permute-start(bf16[1024,512]{1,0:T(8,128)(2,1)S(1)} %add_convert_fusion.1), channel_id=1, source_target_pairs={{0,4},{4,8},{8,12},{12,16},{16,20},{20,24},{24,28},{28,32},{32,36}... | collective-permute-start | bytes 3145736 | tf_op jit(solution)/shard_map/ppermute | solution.py:15
  331.1 1.4 copy-start.6
  453.8 4.2 copy-start.5
  455.6 27.7 %collective-permute-start.6 = (bf16[1024,512]{1,0:T(8,128)(2,1)}, bf16[1024,512]{1,0:T(8,128)(2,1)}, u32[]{:S(2)}, u32[]{:S(2)}) collective-permute-start(bf16[1024,512]{1,0:T(8,128)(2,1)} %get-tuple-element.13), channel_id=1, source_target_pairs={{4,0},{8,4},{12,8},{16,12},{20,16},{24,20},{28,24},{32,28},{36,32}... | collective-permute-start | bytes 3145736 | tf_op jit(solution)/shard_map/ppermute | solution.py:36
  455.9 27.4 %collective-permute-start.8 = (bf16[1024,512]{1,0:T(8,128)(2,1)}, bf16[1024,512]{1,0:T(8,128)(2,1)}, u32[]{:S(2)}, u32[]{:S(2)}) collective-permute-start(bf16[1024,512]{1,0:T(8,128)(2,1)} %get-tuple-element.14), channel_id=1, source_target_pairs={{0,64},{64,0},{4,68},{68,4},{8,72},{72,8},{12,76},{76,12},{16,80},... | collective-permute-start | bytes 3145736 | tf_op jit(solution)/shard_map/ppermute | solution.py:30
  456.3 28.4 %collective-permute-start.7 = (bf16[1024,512]{1,0:T(8,128)(2,1)}, bf16[1024,512]{1,0:T(8,128)(2,1)}, u32[]{:S(2)}, u32[]{:S(2)}) collective-permute-start(bf16[1024,512]{1,0:T(8,128)(2,1)} %get-tuple-element.15), channel_id=1, source_target_pairs={{124,0},{0,4},{4,8},{8,12},{12,16},{16,20},{20,24},{24,28},{28,32}... | collective-permute-start | bytes 3145736 | tf_op jit(solution)/shard_map/ppermute | solution.py:36
  473.2 5.0 copy-start.3
  473.2 8.0 %copy-start.11 = (f32[1024,16]{0,1:T(8,128)S(1)}, f32[1024,16]{0,1:T(8,128)}, u32[]{:S(2)}) copy-start(f32[1024,16]{0,1:T(8,128)} %copy-done.10) | copy-start | bytes 196612
  473.2 8.0 %copy-start.14 = (f32[16,32]{1,0:T(8,128)S(1)}, f32[16,32]{1,0:T(8,128)}, u32[]{:S(2)}) copy-start(f32[16,32]{1,0:T(8,128)} %copy-done.13) | copy-start | bytes 6148
  478.2 3.1 copy-start.4
  478.2 3.1 copy-start.7
  481.3 3.4 copy-start.8
  495.3 88.6 %copy-start.1 = (f32[822,32]{0,1:T(8,128)S(1)}, f32[822,32]{0,1:T(8,128)}, u32[]{:S(2)}) copy-start(f32[822,32]{0,1:T(8,128)} %param.17) | copy-start | bytes 315652
where the time goes:
time: 595 us; the launch traced here: 584 us
  local copies, waits for them, and re-layouts  279 us (47%)
  other arithmetic  123 us (21%)
  blocking collectives  85.4 us (14%)
  matrix products  42 us (7%)
  waiting for transfers between devices  30.7 us (5%)
  starting transfers between devices  22.8 us (4%)
    gather x4, local copies, waits for them, and re-layouts, run_layer(): gathered = jnp.take(extended, edge_tiles[:, 0, :], axis=0)  97.8 us
    psum x1, blocking collectives, reduce_grads(): return lax.psum((values[0], values[1]), ('node', 'query'))  85.4 us
    gather x2, local copies, waits for them, and re-layouts, run_layer(): rel_scales = jnp.take(rel_vectors[layer_index], edge_tiles[:, 2, :], axis=0)  55.5 us
    scatter-add x1, other arithmetic, contributions(): jax.ops.segment_sum(edge_terms, segment_ids, num_segments=slot_count + 1)  52.9 us
    unnamed x46, local copies, waits for them, and re-layouts  23.4 us
    convert_element_type x2, other arithmetic, run_layer(): message = (gathered.reshape(tile_count, slot_total, query_count, DIM) * r...  19.4 us
    add x4, local copies, waits for them, and re-layouts, run_layer(): mixed_in = boundary.astype(jnp.float32) + summed  18 us
    mul x1, other arithmetic, contributions(): per_edge.reshape(tile_count, slot_total, col_count // DIM, DIM)  17.8 us
  transfers between devices with their start and end apart: 9, of which 4 were waited for; matrix products, arithmetic and copies ran while one was open for 23% of the time, Pallas kernels for 0%

commit v1 on v0

v1 whole, which is shorter than its diff:
```python
import functools

import jax
import jax.numpy as jnp
from jax import lax
from jax.experimental import pallas as pl
from jax.experimental.pallas import tpu as pltpu
from jax.sharding import PartitionSpec as P

DIM = 32
LANES = 128
TILE = 64
F32 = jnp.float32
BF16 = jnp.bfloat16
MESH = pl.DeviceIdType.MESH
VMEM_BYTES = 56 << 20


def split_dot(left, right_high, right_low):
    high = left.astype(BF16)
    low = (left - high.astype(F32)).astype(BF16)
    total = jnp.dot(high, right_high, preferred_element_type=F32)
    total += jnp.dot(low, right_high, preferred_element_type=F32)
    return total + jnp.dot(high, right_low, preferred_element_type=F32)


def split_pair(matrix):
    high = matrix.astype(BF16)
    return high, (matrix - high.astype(F32)).astype(BF16)


def spread_rows(target, first, block):
    rows, cols = block.shape
    count = cols // LANES
    for c in range(count):
        target[pl.ds(first * count + c, rows, stride=count), :] = block[:, c * LANES : (c + 1) * LANES]


def spread_relations(target, rel_ref):
    wide = jnp.concatenate([rel_ref[...]] * (LANES // DIM), axis=1)
    rows = wide.shape[0]
    for c in range(4):
        target[pl.ds(c, rows, stride=4), :] = wide


def block_sums(product):
    rows = lax.broadcasted_iota(jnp.int32, (LANES, LANES), 0) // DIM
    cols = lax.broadcasted_iota(jnp.int32, (LANES, LANES), 1) // DIM
    kept = jnp.where(rows == cols, product, 0.0)
    folded = kept[0:32] + kept[32:64] + kept[64:96] + kept[96:128]
    folded = fold_lanes(folded)
    lane = lax.broadcasted_iota(jnp.int32, (8, LANES), 1) // DIM
    packed = jnp.where(lane == 0, folded[0:8], 0.0)
    for k in range(1, 4):
        packed = jnp.where(lane == k, folded[8 * k : 8 * k + 8], packed)
    return packed


def fold_lanes(values):
    values = values + pltpu.roll(values, 64, 1)
    return values + pltpu.roll(values, 32, 1)


def gather_tile(tile, slots_ref, rels_ref, win_ref, rel_ref, message_ref, slot_total, unroll):
    def block(b, carry):
        base = tile * slot_total + b * unroll
        for u in range(unroll):
            slot = pl.multiple_of(slots_ref[base + u], 4)
            rel = pl.multiple_of(rels_ref[base + u], 4)
            place = pl.multiple_of((b * unroll + u) * 4, 4)
            message_ref[pl.ds(place, 4), :] = win_ref[pl.ds(slot, 4), :] * rel_ref[pl.ds(rel, 4), :]
        return carry

    lax.fori_loop(0, slot_total // unroll, block, 0)


def sum_messages(
    first_row, slots_ref, rels_ref, targets_ref, head_ref, query_ref, win_ref, rel_ref, message_ref, mixed_ref
):
    tiles, unused, slot_total = targets_ref.shape

    def tile_step(tile, carry):
        gather_tile(tile, slots_ref, rels_ref, win_ref, rel_ref, message_ref, slot_total, 32)
        onehot = (targets_ref[tile] == lax.broadcasted_iota(jnp.int32, (TILE, slot_total), 0)).astype(BF16)
        row = pl.multiple_of(tile * TILE, TILE)
        ids = first_row + row + lax.broadcasted_iota(jnp.int32, (TILE, LANES), 0)
        for c in range(4):
            cols = slice(c * LANES, (c + 1) * LANES)
            message = message_ref[pl.ds(c, slot_total, stride=4), :].astype(BF16)
            summed = jnp.dot(onehot, message, preferred_element_type=F32)
            start = jnp.where(ids == head_ref[:, cols], query_ref[:, cols], 0.0)
            mixed_ref[pl.ds(row, TILE), cols] = start + summed
        return carry

    lax.fori_loop(0, tiles, tile_step, 0)


def layer_zero_kernel(
    slots_ref, rels_ref, targets_ref, head_ref, query_ref, rel_in, low_ref, own_ref, high_ref, mirror_ref,
    weight_ref, bias_ref, state_out, mixed_out, slope_out, win_ref, rel_ref, message_ref, mixed_ref,
):
    rows = own_ref.shape[0]
    spread_relations(rel_ref, rel_in)
    for quarter, block in enumerate((low_ref, own_ref, high_ref, mirror_ref)):
        def fill(i, carry, quarter=quarter, block=block):
            at = pl.multiple_of(i * TILE, TILE)
            spread_rows(win_ref, quarter * rows + at, block[pl.ds(at, TILE), :].astype(F32))
            return carry

        lax.fori_loop(0, rows // TILE, fill, 0)
    first_row = lax.axis_index("node") * rows
    sum_messages(
        first_row, slots_ref, rels_ref, targets_ref, head_ref, query_ref, win_ref, rel_ref, message_ref, mixed_ref
    )
    weight_high, weight_low = split_pair(weight_ref[...])

    def finish(i, carry):
        at = pl.ds(pl.multiple_of(i * 256, 256), 256)
        for half in range(2):
            cols = slice(half * 256, half * 256 + 256)
            mixed = mixed_ref[at, cols]
            update = split_dot(mixed, weight_high, weight_low) + bias_ref[...]
            sigma = jax.nn.sigmoid(update)
            state_out[at, cols] = (own_ref[at, cols].astype(F32) + update * sigma).astype(BF16)
            slope_out[at, cols] = sigma * (1.0 + update * (1.0 - sigma))
            mixed_out[at, cols] = mixed.astype(BF16)
        return carry

    lax.fori_loop(0, rows // 256, finish, 0)


def layer_one_kernel(
    slots_ref, rels_ref, places_ref, targets_ref, head_ref, query_ref, rel_in, low_ref, own_ref, high_ref, mirror_ref,
    weight_ref, back_ref, bias_ref, cot_ref, state_out, own_out, low_out, high_out, mirror_out, sums_out,
    win_ref, second_ref, rel_ref, message_ref, mixed_ref, grad_ref,
):
    rows = own_ref.shape[0]
    spread_relations(rel_ref, rel_in)
    for quarter, block in enumerate((low_ref, own_ref, high_ref, mirror_ref)):
        def fill(i, carry, quarter=quarter, block=block):
            at = pl.multiple_of(i * TILE, TILE)
            spread_rows(win_ref, quarter * rows + at, block[pl.ds(at, TILE), :].astype(F32))
            return carry

        lax.fori_loop(0, rows // TILE, fill, 0)
    first_row = lax.axis_index("node") * rows
    sum_messages(
        first_row, slots_ref, rels_ref, targets_ref, head_ref, query_ref, win_ref, rel_ref, message_ref, mixed_ref
    )
    weight_high, weight_low = split_pair(weight_ref[...])
    back_high, back_low = split_pair(back_ref[...])

    def finish(i, carry):
        product, bias_sum = carry
        start = pl.multiple_of(i * 256, 256)
        at = pl.ds(start, 256)
        for half in range(2):
            cols = slice(half * 256, half * 256 + 256)
            mixed = mixed_ref[at, cols]
            update = split_dot(mixed, weight_high, weight_low) + bias_ref[...]
            sigma = jax.nn.sigmoid(update)
            state_out[at, cols] = (own_ref[at, cols].astype(F32) + update * sigma).astype(BF16)
            grad = cot_ref[at, cols].astype(F32) * (sigma * (1.0 + update * (1.0 - sigma)))
            back = split_dot(grad, back_high, back_low).astype(BF16).astype(F32)
            for c in range(2):
                grad_ref[pl.ds(start * 4 + half * 2 + c, 256, stride=4), :] = back[:, c * LANES : (c + 1) * LANES]
                part = slice(c * LANES, (c + 1) * LANES)
                product += lax.dot_general(
                    mixed[:, part].astype(BF16), grad[:, part].astype(BF16),
                    (((0,), (0,)), ((), ())), preferred_element_type=F32,
                )
                bias_sum += jnp.sum(grad[:, part], axis=0, keepdims=True)
        return product, bias_sum

    product, bias_sum = lax.fori_loop(
        0, rows // 256, finish, (jnp.zeros((LANES, LANES), F32), jnp.zeros((1, LANES), F32))
    )
    sums_out[0:8, :] = block_sums(product)
    sums_out[8:16, :] = jnp.broadcast_to(fold_lanes(jnp.broadcast_to(bias_sum, (8, LANES))), (8, LANES))

    def clear(i, carry):
        at = pl.ds(pl.multiple_of(i * 256, 256), 256)
        win_ref[at, :] = jnp.zeros((256, LANES), F32)
        second_ref[at, :] = jnp.zeros((256, LANES), F32)
        return carry

    lax.fori_loop(0, rows * 16 // 256, clear, 0)
    edges = slots_ref.shape[0]
    unroll = 16

    def scatter(b, carry):
        base = b * unroll
        for u in range(unroll):
            total = win_ref if u % 2 == 0 else second_ref
            slot = pl.multiple_of(slots_ref[base + u], 4)
            rel = pl.multiple_of(rels_ref[base + u], 4)
            place = pl.multiple_of(places_ref[base + u], 4)
            term = grad_ref[pl.ds(place, 4), :] * rel_ref[pl.ds(rel, 4), :]
            total[pl.ds(slot, 4), :] = total[pl.ds(slot, 4), :] + term
        return carry

    lax.fori_loop(0, edges // unroll, scatter, 0)
    for quarter, out in enumerate((low_out, own_out, high_out, mirror_out)):
        def collect(i, carry, quarter=quarter, out=out):
            start = pl.multiple_of(i * TILE, TILE)
            for c in range(4):
                at = pl.ds((quarter * rows + start) * 4 + c, TILE, stride=4)
                out[pl.ds(start, TILE), c * LANES : (c + 1) * LANES] = (win_ref[at, :] + second_ref[at, :]).astype(out.dtype)
            return carry

        lax.fori_loop(0, rows // TILE, collect, 0)


def last_kernel(
    cot_ref, own_ref, right_ref, left_ref, mirror_ref, slope_ref, mixed_ref, sums_ref,
    weight_out, bias_out, mine, first_buf, second_buf, first_send, first_recv, second_send, second_recv,
):
    node, query = lax.axis_index("node"), lax.axis_index("query")
    low_node = lax.rem(node, 16)
    half = node // 16
    in_first = half * 4 + query
    barrier = pltpu.get_barrier_semaphore()

    def first_peer(j):
        return {"node": (j // 4) * 16 + low_node, "query": lax.rem(j, 4)}

    def second_peer(j):
        return {"node": half * 16 + j, "query": query}

    for d in range(1, 8):
        pl.semaphore_signal(barrier, inc=1, device_id=first_peer(lax.rem(in_first + d, 8)), device_id_type=MESH)
    for d in range(1, 16):
        pl.semaphore_signal(barrier, inc=1, device_id=second_peer(lax.rem(low_node + d, 16)), device_id_type=MESH)

    rows = cot_ref.shape[0]

    def step(i, carry):
        product, bias_sum = carry
        at = pl.ds(pl.multiple_of(i * 256, 256), 256)
        for c in range(4):
            cols = slice(c * LANES, (c + 1) * LANES)
            state_grad = cot_ref[at, cols].astype(F32) + (
                own_ref[at, cols]
                + right_ref[at, cols].astype(F32)
                + left_ref[at, cols].astype(F32)
                + mirror_ref[at, cols].astype(F32)
            )
            grad = state_grad * slope_ref[at, cols]
            product += lax.dot_general(
                mixed_ref[at, cols], grad.astype(BF16), (((0,), (0,)), ((), ())), preferred_element_type=F32
            )
            bias_sum += jnp.sum(grad, axis=0, keepdims=True)
        return product, bias_sum

    product, bias_sum = lax.fori_loop(
        0, rows // 256, step, (jnp.zeros((LANES, LANES), F32), jnp.zeros((1, LANES), F32))
    )
    bias_zero = fold_lanes(jnp.broadcast_to(bias_sum, (8, LANES)))
    mine[0:8, :] = block_sums(product)
    mine[8:16, :] = sums_ref[0:8, :]
    sub = lax.broadcasted_iota(jnp.int32, (8, LANES), 0)
    mine[16:24, :] = jnp.where(sub == 0, bias_zero, sums_ref[8:16, :])

    pl.semaphore_wait(barrier, 22)

    def stage(buf, send, recv, me, peer, count):
        copies = []
        for d in range(1, count):
            to = lax.rem(me + d, count)
            copy = pltpu.make_async_remote_copy(
                src_ref=mine, dst_ref=buf.at[me], send_sem=send.at[to], recv_sem=recv.at[me],
                device_id=peer(to), device_id_type=MESH,
            )
            copy.start()
            copies.append(copy)
        buf[me] = mine[...]
        for d in range(1, count):
            source = lax.rem(me + d, count)
            pltpu.make_async_remote_copy(
                src_ref=mine, dst_ref=buf.at[source], send_sem=send.at[source], recv_sem=recv.at[source],
                device_id=peer(source), device_id_type=MESH,
            ).wait_recv()
        for copy in copies:
            copy.wait_send()
        total = buf[0]
        for j in range(1, count):
            total = total + buf[j]
        return total

    mine[...] = stage(first_buf, first_send, first_recv, in_first, first_peer, 8)
    total = stage(second_buf, second_send, second_recv, low_node, second_peer, 16)
    for l in range(2):
        packed = total[8 * l : 8 * l + 8, :]
        for k in range(4):
            moved = packed if k == 0 else pltpu.roll(packed, LANES - 32 * k, 1)
            weight_out[l, 8 * k : 8 * k + 8, :] = moved[:, 0:32]
    bias_out[...] = total[16:18, 0:32]


def ring_moves(block, mirror_bit):
    count = lax.axis_size("node")
    forward = [(i, (i + 1) % count) for i in range(count)]
    backward = [((i + 1) % count, i) for i in range(count)]
    low = lax.ppermute(block, "node", forward)
    high = lax.ppermute(block, "node", backward)
    return low, high, across(block, mirror_bit)


def across(block, mirror_bit):
    count = lax.axis_size("node")
    return lax.ppermute(block, "node", [(i, i ^ (1 << mirror_bit)) for i in range(count)])


def block_diagonal(matrix):
    size = 256
    at = lax.iota(jnp.int32, size) // DIM
    return jnp.where(at[:, None] == at[None, :], jnp.tile(matrix, (size // DIM, size // DIM)), 0.0)


def body(
    entity_state, edge_tiles, query_head, query_relation, query_table, rel_vectors, mix_weight, mix_bias, cotangent
):
    rows, cols = entity_state.shape
    tiles, unused, slot_total = edge_tiles.shape
    edges = tiles * slot_total
    mirror_bit = lax.axis_size("node").bit_length() - 2
    rel_rows = rel_vectors.shape[1]
    low, high, mirror = ring_moves(entity_state, mirror_bit)
    slots = (edge_tiles[:, 0, :] * 4).reshape(edges)
    rels = (edge_tiles[:, 2, :] * 4).reshape(edges)
    targets = edge_tiles[:, 1:2, :]
    places = ((edge_tiles[:, 1, :] + TILE * lax.iota(jnp.int32, tiles)[:, None]) * 4).reshape(edges)
    head = jnp.repeat(query_head, DIM)[None, :]
    query_vec = jnp.take(query_table, query_relation, axis=0).astype(BF16).astype(F32).reshape(1, cols)
    bias = jnp.tile(mix_bias, (1, 256 // DIM))
    smem = pl.BlockSpec(memory_space=pltpu.SMEM)
    vmem = pl.BlockSpec(memory_space=pltpu.VMEM)
    params = pltpu.CompilerParams(vmem_limit_bytes=VMEM_BYTES)
    scratch = [
        pltpu.VMEM((rows * 16, LANES), F32),
        pltpu.VMEM((rel_rows * 4, LANES), F32),
        pltpu.VMEM((slot_total * 4, LANES), F32),
        pltpu.VMEM((rows, cols), F32),
    ]
    full = jax.ShapeDtypeStruct((rows, cols), F32)
    half = jax.ShapeDtypeStruct((rows, cols), BF16)
    state_one, mixed_zero, slope_zero = pl.pallas_call(
        layer_zero_kernel,
        out_shape=(half, half, full),
        in_specs=[smem] * 2 + [vmem] * 10,
        out_specs=(vmem,) * 3,
        scratch_shapes=scratch,
        compiler_params=params,
        name="layer_zero",
    )(
        slots, rels, targets, head, query_vec, rel_vectors[0], low, entity_state, high, mirror,
        block_diagonal(mix_weight[0]), bias[0:1],
    )
    low, high, mirror = ring_moves(state_one, mirror_bit)
    state_two, own_terms, low_terms, high_terms, mirror_terms, sums = pl.pallas_call(
        layer_one_kernel,
        out_shape=(half, full, half, half, half, jax.ShapeDtypeStruct((16, LANES), F32)),
        in_specs=[smem] * 3 + [vmem] * 12,
        out_specs=(vmem,) * 6,
        scratch_shapes=[scratch[0]] + scratch + [pltpu.VMEM((rows * 4, LANES), F32)],
        compiler_params=params,
        name="layer_one",
    )(
        slots, rels, places, targets, head, query_vec, rel_vectors[1], low, state_one, high, mirror,
        block_diagonal(mix_weight[1]), block_diagonal(mix_weight[1].T), bias[1:2], cotangent,
    )
    count = lax.axis_size("node")
    from_right = lax.ppermute(low_terms, "node", [((i + 1) % count, i) for i in range(count)])
    from_left = lax.ppermute(high_terms, "node", [(i, (i + 1) % count) for i in range(count)])
    from_mirror = across(mirror_terms, mirror_bit)
    packet = (24, LANES)
    weight_grads, bias_grads = pl.pallas_call(
        last_kernel,
        out_shape=(jax.ShapeDtypeStruct((2, DIM, DIM), F32), jax.ShapeDtypeStruct((2, DIM), F32)),
        in_specs=[vmem] * 8,
        out_specs=(vmem,) * 2,
        scratch_shapes=[
            pltpu.VMEM(packet, F32),
            pltpu.VMEM((8,) + packet, F32),
            pltpu.VMEM((16,) + packet, F32),
            pltpu.SemaphoreType.DMA((8,)),
            pltpu.SemaphoreType.DMA((8,)),
            pltpu.SemaphoreType.DMA((16,)),
            pltpu.SemaphoreType.DMA((16,)),
        ],
        compiler_params=pltpu.CompilerParams(
            vmem_limit_bytes=VMEM_BYTES, collective_id=0, has_side_effects=True
        ),
        name="last_sums",
    )(cotangent, own_terms, from_right, from_left, from_mirror, slope_zero, mixed_zero, sums)
    return state_two, weight_grads, bias_grads


def solution(mesh):
    placed = (
        P("node", "query"),
        P("node", None, None),
        P("query"),
        P("query"),
        P(),
        P(),
        P(),
        P(),
        P("node", "query"),
    )
    return jax.shard_map(
        body, mesh=mesh, in_specs=placed, out_specs=(P("node", "query"), P(), P()), check_vma=False
    )
```

time: 595 us -> 226 us (0.38); the launches traced: 584 us -> 225 us
  local copies, waits for them, and re-layouts: 279 us -> 17.5 us
  other arithmetic: 123 us -> 3.85 us
  Pallas kernels: 0 us -> 114 us
  blocking collectives: 85.4 us -> 0 us
  matrix products: 42 us -> 0 us
  waiting for transfers between devices: 30.7 us -> 70.8 us
    gather x6 -> x1, local copies, waits for them, and re-layouts: 153 us -> 0.58 us  [body(): jnp.take(query_table, query_relation, axis=0).astype(BF16).astype(F32)]
    pallas_call x0 -> x3, Pallas kernels: none -> 114 us  [the longest x1 51.9 us: body(): pl.pallas_call(layer_one_kernel, out_shape=(half, full, half, half, half,...]
    psum x1 -> x0, blocking collectives: 85.4 us -> none  [reduce_grads(): return lax.psum((values[0], values[1]), ('node', 'query'))]
    scatter-add x1 -> x0, other arithmetic: 52.9 us -> none  [contributions(): jax.ops.segment_sum(edge_terms, segment_ids, num_segments=slot_count + 1)]
    dot_general x9 -> x0, matrix products: 42 us -> none  [the longest x2 16 us: run_layer(): jnp.einsum('tre,tec->trc', own_onehot, message, preferred_element_type=jn...]
    ppermute x9, waiting for transfers between devices: 30.7 us -> 70.8 us  [the longest x3 19.5 us: across(): lax.ppermute(block, 'node', [(i, i ^ 1 << mirror_bit) for i in range(coun...]
    reshape x5 -> x0, local copies, waits for them, and re-layouts: 31.7 us -> none  [the longest x1 17.4 us: contributions(): per_edge.reshape(tile_count, slot_total, col_count // DIM, DIM)]
    mul x6 -> x0, local copies, waits for them, and re-layouts: 26.6 us -> none  [the longest x1 17.4 us: contributions(): per_edge.reshape(tile_count, slot_total, col_count // DIM, DIM)]
  transfers between devices with their start and end apart: 9 -> 9, of which waited for: 4 -> 6; matrix products, arithmetic and copies ran while one was open for 23% -> 7% of each run, Pallas kernels for 0% -> 0%
where the time goes in v1:
time: 226 us; the launch traced here: 225 us
  Pallas kernels  114 us (50%)
  waiting for transfers between devices  70.8 us (31%)
  starting transfers between devices  18 us (8%)
  local copies, waits for them, and re-layouts  17.5 us (8%)
  other arithmetic  3.85 us (2%)
    pallas_call x1, Pallas kernels, body(): pl.pallas_call(layer_one_kernel, out_shape=(half, full, half, half, half,...  51.9 us
    pallas_call x1, Pallas kernels, body(): pl.pallas_call(last_kernel, out_shape=(jax.ShapeDtypeStruct((2, DIM, DIM)...  39 us
    pallas_call x1, Pallas kernels, body(): pl.pallas_call(layer_zero_kernel, out_shape=(half, half, full), in_specs=...  23.6 us
    ppermute x3, waiting for transfers between devices, across(): lax.ppermute(block, 'node', [(i, i ^ 1 << mirror_bit) for i in range(coun...  19.5 us
    ppermute x1, waiting for transfers between devices, body(): lax.ppermute(low_terms, 'node', [((i + 1) % count, i) for i in range(coun...  16.9 us
    ppermute x2, waiting for transfers between devices, ring_moves(): low = lax.ppermute(block, 'node', forward)  15 us
    ppermute x2, starting transfers between devices, ring_moves(): high = lax.ppermute(block, 'node', backward)  12.2 us
    ppermute x1, waiting for transfers between devices, body(): lax.ppermute(high_terms, 'node', [(i, (i + 1) % count) for i in range(cou...  10.9 us
  transfers between devices with their start and end apart: 9, of which 6 were waited for; matrix products, arithmetic and copies ran while one was open for 7% of the time, Pallas kernels for 0%

profile of v1, /device:TPU:0, one launch (start us, length us, event | category | flops | bytes accessed | tf_op | source)
XLA Modules:
  0.0 225.4 jit_solution(16051263354623962993)
XLA Ops:
  0.6 9.0 %collective-permute-start.1 = (bf16[1024,512]{1,0:T(8,128)(2,1)}, bf16[1024,512]{1,0:T(8,128)(2,1)S(1)}, u32[]{:S(2)}, u32[]{:S(2)}) collective-permute-start(bf16[1024,512]{1,0:T(8,128)(2,1)} %own_ref.1), channel_id=1, source_target_pairs={{4,0},{8,4},{12,8},{16,12},{20,16},{24,20},{28,24},{32,28},{36,32}... | collective-permute-start | bytes 3145736 | tf_op jit(solution)/shard_map/ppermute | solution.py:305
  10.0 0.7 compare_select_fusion.3
  10.6 0.8 slice_bitcast_fusion.3
  12.1 0.7 broadcast_in_dim.28
  13.4 0.7 slice_bitcast_fusion.1
  14.2 0.8 fusion.2
  15.0 0.6 copy.17.targets_ref
  16.9 1.1 copy.13
  18.6 0.7 compare_and_fusion
  19.3 0.6 reshape.100.query_ref
  19.9 1.0 fusion.1
  20.9 1.0 copy.19
  23.1 1.0 compare_select_fusion
  24.1 8.3 %collective-permute-done.1.high_ref = bf16[1024,512]{1,0:T(8,128)(2,1)S(1)} collective-permute-done((bf16[1024,512]{1,0:T(8,128)(2,1)}, bf16[1024,512]{1,0:T(8,128)(2,1)S(1)}, u32[]{:S(2)}, u32[]{:S(2)}) %collective-permute-start.1) | collective-permute-done | bytes 1048608 | tf_op jit(solution)/shard_map/ppermute | solution.py:305
  32.4 8.0 %collective-permute-done.low_ref = bf16[1024,512]{1,0:T(8,128)(2,1)} collective-permute-done((bf16[1024,512]{1,0:T(8,128)(2,1)}, bf16[1024,512]{1,0:T(8,128)(2,1)}, u32[]{:S(2)}, u32[]{:S(2)}) %collective-permute-start) | collective-permute-done | bytes 1048608 | tf_op jit(solution)/shard_map/ppermute | solution.py:304
  40.4 23.6 %layer_zero.1 = (bf16[1024,512]{1,0:T(8,128)(2,1)}, bf16[1024,512]{1,0:T(8,128)(2,1)}, f32[1024,512]{1,0:T(8,128)}) custom-call(s32[8192]{0:T(1024)} %bitcast.34, s32[8192]{0:T(1024)} %bitcast.36, s32[16,1,512]{2,1,0:T(1,128)} %copy.17.targets_ref, s32[1,512]{1,0:T(1,128)} %broadcast_in_dim_reshape.3.head_ref, f32[1,512]{1,0:T(1,128)} %reshape.100.query_ref, ...), custom_call_target="tpu_custom_call" | custom-call | tf_op jit(solution)/shard_map/layer_zero/pallas_call | solution.py:347
  64.4 3.2 %collective-permute-start.4 = (bf16[1024,512]{1,0:T(8,128)(2,1)}, bf16[1024,512]{1,0:T(8,128)(2,1)S(1)}, u32[]{:S(2)}, u32[]{:S(2)}) collective-permute-start(bf16[1024,512]{1,0:T(8,128)(2,1)} %get-tuple-element.14.own_ref), channel_id=1, source_target_pairs={{4,0},{8,4},{12,8},{16,12},{20,16},{24,20},{28,24},{32,28},{36,32}... | collective-permute-start | bytes 3145736 | tf_op jit(solution)/shard_map/ppermute | solution.py:305
  67.6 0.6 tile.53.bias_ref
  68.3 1.0 copy.18
  69.9 19.5 %collective-permute-done.5.mirror_ref = bf16[1024,512]{1,0:T(8,128)(2,1)S(1)} collective-permute-done((bf16[1024,512]{1,0:T(8,128)(2,1)}, bf16[1024,512]{1,0:T(8,128)(2,1)S(1)}, u32[]{:S(2)}, u32[]{:S(2)}) %collective-permute-start.5) | collective-permute-done | bytes 1048608 | tf_op jit(solution)/shard_map/ppermute | solution.py:311
  89.4 7.0 %collective-permute-done.3.low_ref = bf16[1024,512]{1,0:T(8,128)(2,1)S(1)} collective-permute-done((bf16[1024,512]{1,0:T(8,128)(2,1)}, bf16[1024,512]{1,0:T(8,128)(2,1)S(1)}, u32[]{:S(2)}, u32[]{:S(2)}) %collective-permute-start.3) | collective-permute-done | bytes 1048608 | tf_op jit(solution)/shard_map/ppermute | solution.py:304
  96.5 1.0 copy-done.3
  97.5 51.9 %layer_one.1 = (bf16[1024,512]{1,0:T(8,128)(2,1)}, f32[1024,512]{1,0:T(8,128)}, bf16[1024,512]{1,0:T(8,128)(2,1)}, bf16[1024,512]{1,0:T(8,128)(2,1)}, bf16[1024,512]{1,0:T(8,128)(2,1)}, /*index=5*/f32[16,128]{1,0:T(8,128)}) custom-call(s32[8192]{0:T(1024)} %bitcast.35, s32[8192]{0:T(1024)} %bitcast.37, s32[8192]{0:T(1024)} %add_multiply_fusion.places_ref, ...), custom_call_target="tpu_custom_call" | custom-call | tf_op jit(solution)/shard_map/layer_one/pallas_call | solution.py:360
  149.4 0.7 collective-permute-start.6
  150.0 1.4 collective-permute-start.7
  151.4 3.2 %collective-permute-start.8 = (bf16[1024,512]{1,0:T(8,128)(2,1)}, bf16[1024,512]{1,0:T(8,128)(2,1)S(1)}, u32[]{:S(2)}, u32[]{:S(2)}) collective-permute-start(bf16[1024,512]{1,0:T(8,128)(2,1)} %get-tuple-element.19), channel_id=1, source_target_pairs={{0,64},{4,68},{8,72},{12,76},{16,80},{20,84},{24,88},{28,92},{32,9... | collective-permute-start | bytes 3145736 | tf_op jit(solution)/shard_map/ppermute | solution.py:311
  154.5 16.9 %collective-permute-done.6.right_ref = bf16[1024,512]{1,0:T(8,128)(2,1)S(1)} collective-permute-done((bf16[1024,512]{1,0:T(8,128)(2,1)}, bf16[1024,512]{1,0:T(8,128)(2,1)S(1)}, u32[]{:S(2)}, u32[]{:S(2)}) %collective-permute-start.6) | collective-permute-done | bytes 1048608 | tf_op jit(solution)/shard_map/ppermute | solution.py:373
  171.5 10.9 %collective-permute-done.7.left_ref = bf16[1024,512]{1,0:T(8,128)(2,1)S(1)} collective-permute-done((bf16[1024,512]{1,0:T(8,128)(2,1)}, bf16[1024,512]{1,0:T(8,128)(2,1)S(1)}, u32[]{:S(2)}, u32[]{:S(2)}) %collective-permute-start.7) | collective-permute-done | bytes 1048608 | tf_op jit(solution)/shard_map/ppermute | solution.py:374
  182.4 1.0 copy-done.5
  183.7 39.0 %last_sums.1 = (f32[2,32,32]{2,1,0:T(8,128)}, f32[2,32]{1,0:T(2,128)}) custom-call(bf16[1024,512]{1,0:T(8,128)(2,1)} %cot_ref.3, f32[1024,512]{1,0:T(8,128)} %get-tuple-element.16.own_ref, bf16[1024,512]{1,0:T(8,128)(2,1)} %copy-done.4, bf16[1024,512]{1,0:T(8,128)(2,1)} %copy-done.5, bf16[1024,512]{1,0:T(8,128)(2,1)} %copy-done.6, ...), custom_call_target="tpu_custom_call" | custom-call | tf_op jit(solution)/shard_map/last_sums/pallas_call | solution.py:377
  222.7 1.4 copy.25
  224.1 1.2 copy.26
  (42 shorter events, 6.1 us)
Async XLA Ops:
  0.6 31.8 %collective-permute-start.1 = (bf16[1024,512]{1,0:T(8,128)(2,1)}, bf16[1024,512]{1,0:T(8,128)(2,1)S(1)}, u32[]{:S(2)}, u32[]{:S(2)}) collective-permute-start(bf16[1024,512]{1,0:T(8,128)(2,1)} %own_ref.1), channel_id=1, source_target_pairs={{4,0},{8,4},{12,8},{16,12},{20,16},{24,20},{28,24},{32,28},{36,32}... | collective-permute-start | bytes 3145736 | tf_op jit(solution)/shard_map/ppermute | solution.py:305
  9.6 30.8 %collective-permute-start = (bf16[1024,512]{1,0:T(8,128)(2,1)}, bf16[1024,512]{1,0:T(8,128)(2,1)}, u32[]{:S(2)}, u32[]{:S(2)}) collective-permute-start(bf16[1024,512]{1,0:T(8,128)(2,1)} %own_ref.1), channel_id=1, source_target_pairs={{0,4},{4,8},{8,12},{12,16},{16,20},{20,24},{24,28},{28,32},{32,36}... | collective-permute-start | bytes 3145736 | tf_op jit(solution)/shard_map/ppermute | solution.py:304
  9.6 30.8 %collective-permute-start.2 = (bf16[1024,512]{1,0:T(8,128)(2,1)}, bf16[1024,512]{1,0:T(8,128)(2,1)}, u32[]{:S(2)}, u32[]{:S(2)}) collective-permute-start(bf16[1024,512]{1,0:T(8,128)(2,1)} %own_ref.1), channel_id=1, source_target_pairs={{0,64},{4,68},{8,72},{12,76},{16,80},{20,84},{24,88},{28,92},{32,9... | collective-permute-start | bytes 3145736 | tf_op jit(solution)/shard_map/ppermute | solution.py:311
  32.4 8.0 %copy-start = (bf16[1024,512]{1,0:T(8,128)(2,1)}, bf16[1024,512]{1,0:T(8,128)(2,1)S(1)}, u32[]{:S(2)}) copy-start(bf16[1024,512]{1,0:T(8,128)(2,1)S(1)} %collective-permute-done.1.high_ref) | copy-start | bytes 3145732
  40.4 28.9 %copy-start.7 = (s32[16,1,512]{2,1,0:T(1,128)S(1)}, s32[16,1,512]{2,1,0:T(1,128)}, u32[]{:S(2)}) copy-start(s32[16,1,512]{2,1,0:T(1,128)} %copy.17.targets_ref) | copy-start | bytes 98308
  64.1 25.4 %collective-permute-start.5 = (bf16[1024,512]{1,0:T(8,128)(2,1)}, bf16[1024,512]{1,0:T(8,128)(2,1)S(1)}, u32[]{:S(2)}, u32[]{:S(2)}) collective-permute-start(bf16[1024,512]{1,0:T(8,128)(2,1)} %get-tuple-element.14.own_ref), channel_id=1, source_target_pairs={{0,64},{4,68},{8,72},{12,76},{16,80},{20,84},{24,88},{28,92},{32,9... | collective-permute-start | bytes 3145736 | tf_op jit(solution)/shard_map/ppermute | solution.py:311
  64.4 25.0 %collective-permute-start.4 = (bf16[1024,512]{1,0:T(8,128)(2,1)}, bf16[1024,512]{1,0:T(8,128)(2,1)S(1)}, u32[]{:S(2)}, u32[]{:S(2)}) collective-permute-start(bf16[1024,512]{1,0:T(8,128)(2,1)} %get-tuple-element.14.own_ref), channel_id=1, source_target_pairs={{4,0},{8,4},{12,8},{16,12},{20,16},{24,20},{28,24},{32,28},{36,32}... | collective-permute-start | bytes 3145736 | tf_op jit(solution)/shard_map/ppermute | solution.py:305
  67.5 28.9 %collective-permute-start.3 = (bf16[1024,512]{1,0:T(8,128)(2,1)}, bf16[1024,512]{1,0:T(8,128)(2,1)S(1)}, u32[]{:S(2)}, u32[]{:S(2)}) collective-permute-start(bf16[1024,512]{1,0:T(8,128)(2,1)} %get-tuple-element.14.own_ref), channel_id=1, source_target_pairs={{0,4},{4,8},{8,12},{12,16},{16,20},{20,24},{24,28},{28,32},{32,36}... | collective-permute-start | bytes 3145736 | tf_op jit(solution)/shard_map/ppermute | solution.py:304
  89.4 7.0 %copy-start.1 = (bf16[1024,512]{1,0:T(8,128)(2,1)}, bf16[1024,512]{1,0:T(8,128)(2,1)S(1)}, u32[]{:S(2)}) copy-start(bf16[1024,512]{1,0:T(8,128)(2,1)S(1)} %collective-permute-done.5.mirror_ref) | copy-start | bytes 3145732
  89.4 7.0 %copy-start.2 = (bf16[1024,512]{1,0:T(8,128)(2,1)}, bf16[1024,512]{1,0:T(8,128)(2,1)S(1)}, u32[]{:S(2)}) copy-start(bf16[1024,512]{1,0:T(8,128)(2,1)S(1)} %collective-permute-done.4.high_ref) | copy-start | bytes 3145732
  96.5 1.0 copy-start.3
  149.4 22.1 %collective-permute-start.6 = (bf16[1024,512]{1,0:T(8,128)(2,1)}, bf16[1024,512]{1,0:T(8,128)(2,1)S(1)}, u32[]{:S(2)}, u32[]{:S(2)}) collective-permute-start(bf16[1024,512]{1,0:T(8,128)(2,1)} %get-tuple-element.17), channel_id=1, source_target_pairs={{4,0},{8,4},{12,8},{16,12},{20,16},{24,20},{28,24},{32,28},{36,32}... | collective-permute-start | bytes 3145736 | tf_op jit(solution)/shard_map/ppermute | solution.py:373
  150.0 32.4 %collective-permute-start.7 = (bf16[1024,512]{1,0:T(8,128)(2,1)}, bf16[1024,512]{1,0:T(8,128)(2,1)S(1)}, u32[]{:S(2)}, u32[]{:S(2)}) collective-permute-start(bf16[1024,512]{1,0:T(8,128)(2,1)} %get-tuple-element.18), channel_id=1, source_target_pairs={{0,4},{4,8},{8,12},{12,16},{16,20},{20,24},{24,28},{28,32},{32,36}... | collective-permute-start | bytes 3145736 | tf_op jit(solution)/shard_map/ppermute | solution.py:374
  151.4 31.0 %collective-permute-start.8 = (bf16[1024,512]{1,0:T(8,128)(2,1)}, bf16[1024,512]{1,0:T(8,128)(2,1)S(1)}, u32[]{:S(2)}, u32[]{:S(2)}) collective-permute-start(bf16[1024,512]{1,0:T(8,128)(2,1)} %get-tuple-element.19), channel_id=1, source_target_pairs={{0,64},{4,68},{8,72},{12,76},{16,80},{20,84},{24,88},{28,92},{32,9... | collective-permute-start | bytes 3145736 | tf_op jit(solution)/shard_map/ppermute | solution.py:311
  171.5 10.9 %copy-start.4 = (bf16[1024,512]{1,0:T(8,128)(2,1)}, bf16[1024,512]{1,0:T(8,128)(2,1)S(1)}, u32[]{:S(2)}) copy-start(bf16[1024,512]{1,0:T(8,128)(2,1)S(1)} %collective-permute-done.6.right_ref) | copy-start | bytes 3145732
  182.4 1.1 copy-start.5
  182.4 1.3 copy-start.6

commit v2 on v1

v2 whole, which is shorter than its diff:
```python
import jax
import jax.numpy as jnp
from jax import lax
from jax.experimental import pallas as pl
from jax.experimental.pallas import tpu as pltpu
from jax.sharding import PartitionSpec as P

DIM = 32
LANES = 128
TILE = 64
CHUNK = 128
CHUNKS = 8
RING = 16
F32 = jnp.float32
BF16 = jnp.bfloat16
MESH = pl.DeviceIdType.MESH
VMEM_BYTES = 58 << 20


def split_pair(matrix):
    high = matrix.astype(BF16)
    return high, (matrix - high.astype(F32)).astype(BF16)


def split_dot(left, right_high, right_low, right_dim=0):
    dims = (((1,), (right_dim,)), ((), ()))
    high, low = split_pair(left)
    total = lax.dot_general(high, right_high, dims, preferred_element_type=F32)
    total += lax.dot_general(low, right_high, dims, preferred_element_type=F32)
    return total + lax.dot_general(high, right_low, dims, preferred_element_type=F32)


def spread_rows(target, first, block):
    rows, cols = block.shape
    flat = target.reshape(target.shape[0] * 4, LANES)
    for c in range(4):
        flat[pl.ds(first * 4 + c, rows, stride=4), :] = block[:, c * LANES : (c + 1) * LANES]


def spread_relations(target, columns_ref):
    count = columns_ref.shape[1]
    flat = target.reshape(target.shape[0] * 4, LANES)
    for start in range(0, count, LANES):
        width = min(LANES, count - start)
        wide = jnp.concatenate([columns_ref[:, start : start + width]] * 4, axis=0).T
        for c in range(4):
            flat[pl.ds(start * 4 + c, width, stride=4), :] = wide


def block_diagonal(matrix):
    row = jnp.concatenate([matrix] * 8, axis=1)
    wide = jnp.concatenate([row] * 8, axis=0)
    rows = lax.broadcasted_iota(jnp.int32, (256, 256), 0) // DIM
    cols = lax.broadcasted_iota(jnp.int32, (256, 256), 1) // DIM
    return jnp.where(rows == cols, wide, 0.0)


def fold_lanes(values):
    values = values + pltpu.roll(values, 64, 1)
    return values + pltpu.roll(values, 32, 1)


def block_sums(product):
    rows = lax.broadcasted_iota(jnp.int32, (LANES, LANES), 0) // DIM
    cols = lax.broadcasted_iota(jnp.int32, (LANES, LANES), 1) // DIM
    kept = jnp.where(rows == cols, product, 0.0)
    folded = fold_lanes(kept[0:32] + kept[32:64] + kept[64:96] + kept[96:128])
    lane = lax.broadcasted_iota(jnp.int32, (8, LANES), 1) // DIM
    packed = jnp.where(lane == 0, folded[0:8], 0.0)
    for k in range(1, 4):
        packed = jnp.where(lane == k, folded[8 * k : 8 * k + 8], packed)
    return packed


def product_of(left, right):
    return lax.dot_general(left, right, (((0,), (0,)), ((), ())), preferred_element_type=F32)


def chunk_rows(k):
    return pl.ds(pl.multiple_of(k * CHUNK, CHUNK), CHUNK)


def ring_targets():
    node = lax.axis_index("node")
    position = lax.rem(node, RING)
    plane = node - position
    after = plane + lax.rem(position + 1, RING)
    before = plane + lax.rem(position + RING - 1, RING)
    across = lax.rem(node + RING, 2 * RING)
    return node, position, (after, before, across)


def sum_chunk(k, first_row, edges_s, edges_v, head_ref, query_ref, win_ref, rel_ref, message_ref, mixed_ref):
    slot_total = edges_v.shape[2]
    unroll = 32

    def tile_step(j, carry):
        tile = 2 * k + j

        def block(b, carry):
            for u in range(unroll):
                at = b * unroll + u
                place = pl.multiple_of(at * 4, 4)
                message_ref[pl.ds(place, 4), :] = win_ref[edges_s[0, tile, at]] * rel_ref[edges_s[2, tile, at]]
            return carry

        lax.fori_loop(0, slot_total // unroll, block, 0)
        targets = edges_v[1, pl.ds(tile, 1), :]
        onehot = (targets == lax.broadcasted_iota(jnp.int32, (TILE, slot_total), 0)).astype(BF16)
        row = pl.multiple_of(j * TILE, TILE)
        ids = first_row + tile * TILE + lax.broadcasted_iota(jnp.int32, (TILE, LANES), 0)
        for c in range(4):
            cols = slice(c * LANES, (c + 1) * LANES)
            message = message_ref[pl.ds(c, slot_total, stride=4), :].astype(BF16)
            summed = jnp.dot(onehot, message, preferred_element_type=F32)
            start = jnp.where(ids == head_ref[:, cols], query_ref[:, cols], 0.0)
            mixed_ref[pl.ds(row, TILE), cols] = start + summed
        return carry

    lax.fori_loop(0, 2, tile_step, 0)


def forward_kernel(
    state_hbm, cot_hbm, edges_s, head_s, chosen_s, edges_v, table_t, rel_t, weight_ref, bias_ref,
    state_out, grad_out, mixed_out, slope_out, sums_out,
    own, middle, cot, inbox, win_a, win_b, rel_ref, table_ref, message_ref, mixed_ref, wide_ref, head_ref, query_ref,
    copy_sem, send_sem, recv_sem,
):
    node, position, targets = ring_targets()
    rows = own.shape[0]
    barrier = pltpu.get_barrier_semaphore()
    for target in targets:
        pl.semaphore_signal(barrier, inc=1, device_id={"node": target}, device_id_type=MESH)
    own_copy = pltpu.make_async_copy(state_hbm, own, copy_sem.at[0])
    cot_copy = pltpu.make_async_copy(cot_hbm, cot, copy_sem.at[1])
    own_copy.start()
    cot_copy.start()
    pl.semaphore_wait(barrier, 3)

    def piece(layer, way, k, source):
        return pltpu.make_async_remote_copy(
            src_ref=source.at[chunk_rows(k), :],
            dst_ref=inbox.at[layer, way, chunk_rows(k), :],
            send_sem=send_sem.at[layer, way, k],
            recv_sem=recv_sem.at[layer, way, k],
            device_id={"node": targets[way]},
            device_id_type=MESH,
        )

    def send_chunk(layer, k, source):
        piece(layer, 2, k, source).start()

        @pl.when(position != RING - 1)
        def _():
            piece(layer, 0, k, source).start()

        @pl.when(position != 0)
        def _():
            piece(layer, 1, k, source).start()

    def relay_chunk(layer, k):
        mirrored = inbox.at[layer, 2]
        piece(layer, 2, k, mirrored).wait_recv()

        @pl.when(position == RING - 1)
        def _():
            piece(layer, 0, k, mirrored).start()

        @pl.when(position == 0)
        def _():
            piece(layer, 1, k, mirrored).start()

    def fill(win, quarter, k, block):
        spread_rows(win, quarter * rows + k * CHUNK, block.astype(F32))

    def take_mirror(layer, win, k):
        relay_chunk(layer, k)
        fill(win, 3, k, inbox[layer, 2, chunk_rows(k), :])

    def take_sides(layer, win, k):
        for way, quarter in ((0, 0), (1, 2)):
            piece(layer, way, k, own).wait_recv()
            fill(win, quarter, k, inbox[layer, way, chunk_rows(k), :])

    def each(count, step):
        def run(i, carry):
            step(i)
            return carry

        lax.fori_loop(0, count, run, 0)

    each(CHUNKS, lambda k: send_chunk(0, k, state_hbm))

    spread_relations(table_ref, table_t)
    spread_relations(rel_ref, rel_t.at[0])
    lane = lax.broadcasted_iota(jnp.int32, (1, LANES), 1) // DIM
    for c in range(4):
        heads = jnp.zeros((1, LANES), jnp.int32)
        vectors = jnp.zeros((1, LANES), F32)
        for k in range(4):
            heads = jnp.where(lane == k, head_s[4 * c + k], heads)
            vectors = jnp.where(lane == k, table_ref[chosen_s[4 * c + k]][0:1], vectors)
        head_ref[:, c * LANES : (c + 1) * LANES] = heads
        query_ref[:, c * LANES : (c + 1) * LANES] = vectors.astype(BF16).astype(F32)
    for layer in range(2):
        high, low = split_pair(block_diagonal(weight_ref[layer]))
        wide_ref[2 * layer] = high
        wide_ref[2 * layer + 1] = low
    bias_zero = jnp.concatenate([bias_ref[0:1, :]] * 8, axis=1)
    bias_one = jnp.concatenate([bias_ref[1:2, :]] * 8, axis=1)
    first_row = node * rows

    own_copy.wait()
    each(CHUNKS, lambda k: fill(win_a, 1, k, own[chunk_rows(k), :]))
    each(CHUNKS, lambda k: take_mirror(0, win_a, k))
    each(CHUNKS, lambda k: take_sides(0, win_a, k))

    def zero_step(k):
        sum_chunk(k, first_row, edges_s, edges_v, head_ref, query_ref, win_a, rel_ref, message_ref, mixed_ref)
        at = chunk_rows(k)
        for half in range(2):
            cols = slice(half * 256, half * 256 + 256)
            mixed = mixed_ref[:, cols]
            update = split_dot(mixed, wide_ref[0], wide_ref[1]) + bias_zero
            sigma = jax.nn.sigmoid(update)
            middle[at, cols] = (own[at, cols].astype(F32) + update * sigma).astype(BF16)
            slope_out[at, cols] = sigma * (1.0 + update * (1.0 - sigma))
            mixed_out[at, cols] = mixed.astype(BF16)
        send_chunk(1, k, middle)
        fill(win_b, 1, k, middle[at, :])

        @pl.when(k >= 2)
        def _():
            take_mirror(1, win_b, k - 2)

    each(CHUNKS, zero_step)
    spread_relations(rel_ref, rel_t.at[1])
    each(2, lambda k: take_mirror(1, win_b, k + CHUNKS - 2))
    each(CHUNKS, lambda k: take_sides(1, win_b, k))
    cot_copy.wait()

    def one_step(k, carry):
        product, bias_sum = carry
        sum_chunk(k, first_row, edges_s, edges_v, head_ref, query_ref, win_b, rel_ref, message_ref, mixed_ref)
        at = chunk_rows(k)
        for half in range(2):
            cols = slice(half * 256, half * 256 + 256)
            mixed = mixed_ref[:, cols]
            update = split_dot(mixed, wide_ref[2], wide_ref[3]) + bias_one
            sigma = jax.nn.sigmoid(update)
            state_out[at, cols] = (middle[at, cols].astype(F32) + update * sigma).astype(BF16)
            grad = cot[at, cols].astype(F32) * (sigma * (1.0 + update * (1.0 - sigma)))
            back = split_dot(grad, wide_ref[2], wide_ref[3], 1).astype(BF16).astype(F32)
            for c in range(2):
                part = slice(c * LANES, (c + 1) * LANES)
                grad_out[pl.ds(k * CHUNK * 4 + half * 2 + c, CHUNK, stride=4), :] = back[:, part]
                product += product_of(mixed[:, part].astype(BF16), grad[:, part].astype(BF16))
                bias_sum += jnp.sum(grad[:, part], axis=0, keepdims=True)
        return product, bias_sum

    product, bias_sum = lax.fori_loop(
        0, CHUNKS, one_step, (jnp.zeros((LANES, LANES), F32), jnp.zeros((1, LANES), F32))
    )
    sums_out[0:8, :] = block_sums(product)
    sums_out[8:16, :] = fold_lanes(jnp.broadcast_to(bias_sum, (8, LANES)))
    for layer in range(2):
        for way in range(3):
            each(CHUNKS, lambda k: piece(layer, way, k, own).wait_send())


def scatter_kernel(
    state_in, edges_s, grad_ref, rel_t, state_out, own_out, low_out, high_out, mirror_out,
    first_ref, second_ref, rel_ref, copy_sem,
):
    state_copy = pltpu.make_async_copy(state_in, state_out, copy_sem)
    state_copy.start()
    rows = own_out.shape[0]
    spread_relations(rel_ref, rel_t.at[1])

    def clear(i, carry):
        at = pl.ds(pl.multiple_of(i * TILE, TILE), TILE)
        first_ref[at] = jnp.zeros((TILE, 4, LANES), F32)
        second_ref[at] = jnp.zeros((TILE, 4, LANES), F32)
        return carry

    lax.fori_loop(0, rows * 4 // TILE, clear, 0)
    tiles, slot_total = edges_s.shape[1:]
    unroll = 16

    def tile_step(tile, carry):
        def scatter(b, carry):
            for u in range(unroll):
                total = first_ref if u % 2 == 0 else second_ref
                at = b * unroll + u
                slot = edges_s[0, tile, at]
                place = pl.multiple_of((edges_s[1, tile, at] + tile * TILE) * 4, 4)
                total[slot] = total[slot] + grad_ref[pl.ds(place, 4), :] * rel_ref[edges_s[2, tile, at]]
            return carry

        lax.fori_loop(0, slot_total // unroll, scatter, 0)
        return carry

    lax.fori_loop(0, tiles, tile_step, 0)
    flat_first = first_ref.reshape(rows * 16, LANES)
    flat_second = second_ref.reshape(rows * 16, LANES)
    for quarter, out in enumerate((low_out, own_out, high_out, mirror_out)):
        def collect(i, carry, quarter=quarter, out=out):
            start = pl.multiple_of(i * TILE, TILE)
            for c in range(4):
                at = pl.ds((quarter * rows + start) * 4 + c, TILE, stride=4)
                out[pl.ds(start, TILE), c * LANES : (c + 1) * LANES] = (flat_first[at, :] + flat_second[at, :]).astype(
                    out.dtype
                )
            return carry

        lax.fori_loop(0, rows // TILE, collect, 0)
    state_copy.wait()


def last_kernel(
    low_ref, high_ref, mirror_ref, cot_ref, own_ref, slope_ref, mixed_ref, sums_ref,
    weight_out, bias_out,
    passed, inbox, mine, first_buf, second_buf, back_send, back_recv, first_send, first_recv, second_send, second_recv,
):
    node, position, (after, before, across) = ring_targets()
    query = lax.axis_index("query")
    half = node // RING
    in_first = half * 4 + query
    targets = (before, after, across)
    barrier = pltpu.get_barrier_semaphore()

    def first_peer(j):
        return {"node": (j // 4) * RING + position, "query": lax.rem(j, 4)}

    def second_peer(j):
        return {"node": half * RING + j, "query": query}

    for d in range(1, 8):
        pl.semaphore_signal(barrier, inc=1, device_id=first_peer(lax.rem(in_first + d, 8)), device_id_type=MESH)
    for d in range(1, RING):
        pl.semaphore_signal(barrier, inc=1, device_id=second_peer(lax.rem(position + d, RING)), device_id_type=MESH)
    pl.semaphore_wait(barrier, 22)

    def piece(way, k, source):
        return pltpu.make_async_remote_copy(
            src_ref=source.at[chunk_rows(k), :],
            dst_ref=inbox.at[way, chunk_rows(k), :],
            send_sem=back_send.at[way, k],
            recv_sem=back_recv.at[way, k],
            device_id={"node": targets[way]},
            device_id_type=MESH,
        )

    def each(count, step):
        def run(i, carry):
            step(i)
            return carry

        lax.fori_loop(0, count, run, 0)

    at_end = jnp.logical_or(position == 0, position == RING - 1)

    def send_sides(k):
        piece(0, k, low_ref).start()
        piece(1, k, high_ref).start()

        @pl.when(jnp.logical_not(at_end))
        def _():
            piece(2, k, mirror_ref).start()

    each(CHUNKS, send_sides)

    def relay(way, k):
        piece(way, k, low_ref).wait_recv()
        at = chunk_rows(k)
        passed[at, :] = (mirror_ref[at, :].astype(F32) + inbox[way, at, :].astype(F32)).astype(BF16)
        piece(2, k, passed).start()

    @pl.when(position == RING - 1)
    def _():
        each(CHUNKS, lambda k: relay(0, k))

    @pl.when(position == 0)
    def _():
        each(CHUNKS, lambda k: relay(1, k))

    def step(k, carry):
        product, bias_sum = carry

        @pl.when(position != RING - 1)
        def _():
            piece(0, k, low_ref).wait_recv()

        @pl.when(position != 0)
        def _():
            piece(1, k, low_ref).wait_recv()

        piece(2, k, low_ref).wait_recv()
        at = chunk_rows(k)
        for c in range(4):
            cols = slice(c * LANES, (c + 1) * LANES)
            from_after = jnp.where(position == RING - 1, 0.0, inbox[0, at, cols].astype(F32))
            from_before = jnp.where(position == 0, 0.0, inbox[1, at, cols].astype(F32))
            state_grad = cot_ref[at, cols].astype(F32) + (
                own_ref[at, cols] + from_after + from_before + inbox[2, at, cols].astype(F32)
            )
            grad = state_grad * slope_ref[at, cols]
            product += product_of(mixed_ref[at, cols], grad.astype(BF16))
            bias_sum += jnp.sum(grad, axis=0, keepdims=True)
        return product, bias_sum

    product, bias_sum = lax.fori_loop(
        0, CHUNKS, step, (jnp.zeros((LANES, LANES), F32), jnp.zeros((1, LANES), F32))
    )
    mine[0:8, :] = block_sums(product)
    mine[8:16, :] = sums_ref[0:8, :]
    sub = lax.broadcasted_iota(jnp.int32, (8, LANES), 0)
    mine[16:24, :] = jnp.where(sub == 0, fold_lanes(jnp.broadcast_to(bias_sum, (8, LANES))), sums_ref[8:16, :])

    def stage(buf, send, recv, me, peer, count):
        copies = []
        for d in range(1, count):
            to = lax.rem(me + d, count)
            copy = pltpu.make_async_remote_copy(
                src_ref=mine, dst_ref=buf.at[me], send_sem=send.at[to], recv_sem=recv.at[me],
                device_id=peer(to), device_id_type=MESH,
            )
            copy.start()
            copies.append(copy)
        buf[me] = mine[...]
        for d in range(1, count):
            source = lax.rem(me + d, count)
            pltpu.make_async_remote_copy(
                src_ref=mine, dst_ref=buf.at[source], send_sem=send.at[source], recv_sem=recv.at[source],
                device_id=peer(source), device_id_type=MESH,
            ).wait_recv()
        for copy in copies:
            copy.wait_send()
        total = buf[0]
        for j in range(1, count):
            total = total + buf[j]
        return total

    mine[...] = stage(first_buf, first_send, first_recv, in_first, first_peer, 8)
    total = stage(second_buf, second_send, second_recv, position, second_peer, RING)
    for l in range(2):
        packed = total[8 * l : 8 * l + 8, :]
        for k in range(4):
            moved = packed if k == 0 else pltpu.roll(packed, LANES - 32 * k, 1)
            weight_out[l, 8 * k : 8 * k + 8, :] = moved[:, 0:32]
    bias_out[...] = total[16:18, 0:32]
    for way in range(3):
        each(CHUNKS, lambda k: piece(way, k, low_ref).wait_send())


def body(
    entity_state, edge_tiles, query_head, query_relation, query_table, rel_vectors, mix_weight, mix_bias, cotangent
):
    rows, cols = entity_state.shape
    slot_total = edge_tiles.shape[2]
    rel_rows = rel_vectors.shape[1]
    edges = edge_tiles.transpose(1, 0, 2)
    table_t = query_table.T
    rel_t = rel_vectors.transpose(0, 2, 1)
    smem = pl.BlockSpec(memory_space=pltpu.SMEM)
    vmem = pl.BlockSpec(memory_space=pltpu.VMEM)
    anywhere = pl.BlockSpec(memory_space=pl.ANY)
    full = jax.ShapeDtypeStruct((rows, cols), F32)
    half = jax.ShapeDtypeStruct((rows, cols), BF16)
    tall = jax.ShapeDtypeStruct((rows * 4, LANES), F32)
    window = pltpu.VMEM((rows * 4, 4, LANES), F32)
    relations = pltpu.VMEM((rel_rows, 4, LANES), F32)
    state_two, grad_mixed, mixed_zero, slope_zero, sums = pl.pallas_call(
        forward_kernel,
        out_shape=(half, tall, half, full, jax.ShapeDtypeStruct((16, LANES), F32)),
        in_specs=[anywhere] * 2 + [smem] * 3 + [vmem] * 5,
        out_specs=(vmem,) * 5,
        scratch_shapes=[
            pltpu.VMEM((rows, cols), BF16),
            pltpu.VMEM((rows, cols), BF16),
            pltpu.VMEM((rows, cols), BF16),
            pltpu.VMEM((2, 3, rows, cols), BF16),
            window,
            window,
            relations,
            relations,
            pltpu.VMEM((slot_total * 4, LANES), F32),
            pltpu.VMEM((CHUNK, cols), F32),
            pltpu.VMEM((4, 256, 256), BF16),
            pltpu.VMEM((1, cols), jnp.int32),
            pltpu.VMEM((1, cols), F32),
            pltpu.SemaphoreType.DMA((2,)),
            pltpu.SemaphoreType.DMA((2, 3, CHUNKS)),
            pltpu.SemaphoreType.DMA((2, 3, CHUNKS)),
        ],
        compiler_params=pltpu.CompilerParams(
            vmem_limit_bytes=VMEM_BYTES, collective_id=0, has_side_effects=True
        ),
        name="two_layers",
    )(
        entity_state, cotangent, edges, query_head, query_relation, edges, table_t, rel_t, mix_weight, mix_bias
    )
    state_out, own_terms, low_terms, high_terms, mirror_terms = pl.pallas_call(
        scatter_kernel,
        out_shape=(half, full, half, half, half),
        in_specs=[anywhere, smem, vmem, vmem],
        out_specs=(anywhere,) + (vmem,) * 4,
        scratch_shapes=[window, window, relations, pltpu.SemaphoreType.DMA],
        compiler_params=pltpu.CompilerParams(vmem_limit_bytes=VMEM_BYTES),
        name="scatter_terms",
    )(state_two, edges, grad_mixed, rel_t)
    packet = (24, LANES)
    weight_grads, bias_grads = pl.pallas_call(
        last_kernel,
        out_shape=(jax.ShapeDtypeStruct((2, DIM, DIM), F32), jax.ShapeDtypeStruct((2, DIM), F32)),
        in_specs=[vmem] * 8,
        out_specs=(vmem,) * 2,
        scratch_shapes=[
            pltpu.VMEM((rows, cols), BF16),
            pltpu.VMEM((3, rows, cols), BF16),
            pltpu.VMEM(packet, F32),
            pltpu.VMEM((8,) + packet, F32),
            pltpu.VMEM((RING,) + packet, F32),
            pltpu.SemaphoreType.DMA((3, CHUNKS)),
            pltpu.SemaphoreType.DMA((3, CHUNKS)),
            pltpu.SemaphoreType.DMA((8,)),
            pltpu.SemaphoreType.DMA((8,)),
            pltpu.SemaphoreType.DMA((RING,)),
            pltpu.SemaphoreType.DMA((RING,)),
        ],
        compiler_params=pltpu.CompilerParams(
            vmem_limit_bytes=VMEM_BYTES, collective_id=1, has_side_effects=True
        ),
        name="last_sums",
    )(low_terms, high_terms, mirror_terms, cotangent, own_terms, slope_zero, mixed_zero, sums)
    return state_out, weight_grads, bias_grads


def solution(mesh):
    placed = (
        P("node", "query"),
        P("node", None, None),
        P("query"),
        P("query"),
        P(),
        P(),
        P(),
        P(),
        P("node", "query"),
    )
    return jax.shard_map(
        body, mesh=mesh, in_specs=placed, out_specs=(P("node", "query"), P(), P()), check_vma=False
    )
```

time: 226 us -> 251 us (1.11)
  Pallas kernels: 114 us -> 247 us
  waiting for transfers between devices: 70.8 us -> 0 us
  starting transfers between devices: 18 us -> 0 us
  local copies, waits for them, and re-layouts: 17.5 us -> 2.6 us
  other arithmetic: 3.85 us -> 0 us
    pallas_call x2, Pallas kernels: 75.5 us -> 201 us  [the longest x1 143 us: body(): pl.pallas_call(forward_kernel, out_shape=(half, tall, half, full, jax.Sha...]
    ppermute x9 -> x0, waiting for transfers between devices: 70.8 us -> none  [the longest x3 19.5 us: across(): lax.ppermute(block, 'node', [(i, i ^ 1 << mirror_bit) for i in range(coun...]
    ppermute x9 -> x0, starting transfers between devices: 18 us -> none  [the longest x2 12.2 us: ring_moves(): high = lax.ppermute(block, 'node', backward)]
    pallas_call x1, Pallas kernels: 39 us -> 46.8 us  [body(): pl.pallas_call(last_kernel, out_shape=(jax.ShapeDtypeStruct((2, DIM, DIM)...]
    unnamed x26 -> x2, local copies, waits for them, and re-layouts: 9.97 us -> 2.6 us
    another operation x11 -> x0, local copies, waits for them, and re-layouts: 3.05 us -> none  [the longest x4 1.28 us: body(): bias = jnp.tile(mix_bias, (1, 256 // DIM))]
  transfers between devices with their start and end apart: 9 -> 0, of which waited for: 6 -> 0; matrix products, arithmetic and copies ran while one was open for 7% -> 0% of each run, Pallas kernels for 0% -> 0%
where the time goes in v2:
time: 251 us
  Pallas kernels  247 us (98%)
  local copies, waits for them, and re-layouts  2.6 us (1%)
    pallas_call x1, Pallas kernels, body(): pl.pallas_call(forward_kernel, out_shape=(half, tall, half, full, jax.Sha...  143 us
    pallas_call x1, Pallas kernels, body(): pl.pallas_call(scatter_kernel, out_shape=(half, full, half, half, half),...  57.7 us
    pallas_call x1, Pallas kernels, body(): pl.pallas_call(last_kernel, out_shape=(jax.ShapeDtypeStruct((2, DIM, DIM)...  46.8 us

profile of v2, /device:TPU:0, one launch (start us, length us, event | category | flops | bytes accessed | tf_op | source)
XLA Modules:
  0.0 250.7 jit_solution(6706211312350919615)
XLA Ops:
  0.6 142.9 %two_layers.1 = (bf16[1024,512]{1,0:T(8,128)(2,1)}, f32[4096,128]{1,0:T(8,128)}, bf16[1024,512]{1,0:T(8,128)(2,1)}, f32[1024,512]{1,0:T(8,128)}, f32[16,128]{1,0:T(8,128)}) custom-call(bf16[1024,512]{1,0:T(8,128)(2,1)} %state_hbm.1, bf16[1024,512]{1,0:T(8,128)(2,1)} %cot_ref.1, s32[3,16,512]{2,1,0:T(8,128)} %bitcast.5, s32[16]{0:T(128)} %head_s.1, ...), custom_call_target="tpu_custom_call" | custom-call | tf_op jit(solution)/shard_map/two_layers/pallas_call | solution.py:473
  143.6 57.7 %scatter_terms.1 = (bf16[1024,512]{1,0:T(8,128)(2,1)}, f32[1024,512]{1,0:T(8,128)}, bf16[1024,512]{1,0:T(8,128)(2,1)}, bf16[1024,512]{1,0:T(8,128)(2,1)}, bf16[1024,512]{1,0:T(8,128)(2,1)}) custom-call(bf16[1024,512]{1,0:T(8,128)(2,1)} %get-tuple-element.15.state_in, s32[3,16,512]{2,1,0:T(8,128)} %bitcast.7, f32[4096,128]{1,0:T(8,128)} %get-tuple-element.16.grad_ref, ...), custom_call_target="tpu_custom_call" | custom-call | tf_op jit(solution)/shard_map/scatter_terms/pallas_call | solution.py:503
  201.3 46.8 %last_sums.1 = (f32[2,32,32]{2,1,0:T(8,128)}, f32[2,32]{1,0:T(2,128)}) custom-call(bf16[1024,512]{1,0:T(8,128)(2,1)} %get-tuple-element.18.low_ref, bf16[1024,512]{1,0:T(8,128)(2,1)} %get-tuple-element.19.high_ref, bf16[1024,512]{1,0:T(8,128)(2,1)} %get-tuple-element.20.mirror_ref, bf16[1024,512]{1,0:T(8,128)(2,1)} %cot_ref.1, ...), custom_call_target="tpu_custom_call" | custom-call | tf_op jit(solution)/shard_map/last_sums/pallas_call | solution.py:513
  248.1 1.4 copy.14
  249.5 1.2 copy.15

commit v3 on v2

v3 whole, which is shorter than its diff:
```python
import jax
import jax.numpy as jnp
from jax import lax
from jax.experimental import pallas as pl
from jax.experimental.pallas import tpu as pltpu
from jax.sharding import PartitionSpec as P

DIM = 32
LANES = 128
TILE = 64
CHUNK = 128
CHUNKS = 8
RING = 16
UNROLL = 32
F32 = jnp.float32
BF16 = jnp.bfloat16
MESH = pl.DeviceIdType.MESH
VMEM_BYTES = 58 << 20


def split_pair(matrix):
    high = matrix.astype(BF16)
    return high, (matrix - high.astype(F32)).astype(BF16)


def half_dot(left, right, right_dim):
    return lax.dot_general(left, right, (((1,), (right_dim,)), ((), ())), preferred_element_type=F32)


def split_dot(left, right_high, right_low, right_dim=0):
    high, low = split_pair(left)
    total = half_dot(high, right_high, right_dim) + half_dot(low, right_high, right_dim)
    return total + half_dot(high, right_low, right_dim)


def product_of(left, right):
    return lax.dot_general(left, right, (((0,), (0,)), ((), ())), preferred_element_type=F32)


def each(count, step):
    def run(i, carry):
        step(i)
        return carry

    lax.fori_loop(0, count, run, 0)


def flat(target):
    return target.reshape(target.shape[0] * 4, LANES)


def spread_rows(target, first, block):
    rows = block.shape[0]
    for c in range(4):
        flat(target)[pl.ds(first * 4 + c, rows, stride=4), :] = block[:, c * LANES : (c + 1) * LANES]


def spread_table(target, columns_ref):
    count = columns_ref.shape[1]
    for start in range(0, count, LANES):
        width = min(LANES, count - start)
        wide = jnp.concatenate([columns_ref[:, start : start + width]] * 4, axis=0).T
        for c in range(4):
            flat(target)[pl.ds(start * 4 + c, width, stride=4), :] = wide


def pad_columns(target, columns_ref):
    count = columns_ref.shape[1]
    whole = count // LANES * LANES
    target[:, 0:whole] = columns_ref[:, 0:whole]
    if whole < count:
        rest = jnp.zeros((columns_ref.shape[0], LANES - count + whole), F32)
        target[:, whole : whole + LANES] = jnp.concatenate([columns_ref[:, whole:count], rest], axis=1)


def relation_rows(target, table_ref, edges_v):
    parts = table_ref.shape[1] // LANES
    tiles, slot_total = edges_v.shape[1:]

    def tile_step(tile):
        row = edges_v[2, pl.ds(tile, 1), :]
        for q in range(slot_total // LANES):
            ids = jnp.broadcast_to(row[:, q * LANES : (q + 1) * LANES], (DIM, LANES))
            lane, part = lax.rem(ids, LANES), ids // LANES
            found = jnp.zeros((DIM, LANES), F32)
            for j in range(parts):
                columns = table_ref[:, j * LANES : (j + 1) * LANES]
                found = jnp.where(part == j, jnp.take_along_axis(columns, lane, axis=1), found)
            at = pl.multiple_of(tile * slot_total + q * LANES, LANES)
            target[pl.ds(at, LANES), :] = jnp.concatenate([found] * 4, axis=0).T

    each(tiles, tile_step)


def block_diagonal(matrix):
    row = jnp.concatenate([matrix] * 8, axis=1)
    wide = jnp.concatenate([row] * 8, axis=0)
    rows = lax.broadcasted_iota(jnp.int32, (256, 256), 0) // DIM
    cols = lax.broadcasted_iota(jnp.int32, (256, 256), 1) // DIM
    return jnp.where(rows == cols, wide, 0.0)


def fold_lanes(values):
    values = values + pltpu.roll(values, 64, 1)
    return values + pltpu.roll(values, 32, 1)


def block_sums(product):
    rows = lax.broadcasted_iota(jnp.int32, (LANES, LANES), 0) // DIM
    cols = lax.broadcasted_iota(jnp.int32, (LANES, LANES), 1) // DIM
    kept = jnp.where(rows == cols, product, 0.0)
    folded = fold_lanes(kept[0:32] + kept[32:64] + kept[64:96] + kept[96:128])
    lane = lax.broadcasted_iota(jnp.int32, (8, LANES), 1) // DIM
    packed = jnp.where(lane == 0, folded[0:8], 0.0)
    for k in range(1, 4):
        packed = jnp.where(lane == k, folded[8 * k : 8 * k + 8], packed)
    return packed


def chunk_rows(k):
    return pl.ds(pl.multiple_of(k * CHUNK, CHUNK), CHUNK)


def slot_base(tile, block):
    return (tile // 8 * 4 + block // 4) * 1024 + lax.rem(tile, 8) * LANES + lax.rem(block, 4) * UNROLL


def target_onehot(edges_v, tile):
    targets = edges_v[1, pl.ds(tile, 1), :]
    return (targets == lax.broadcasted_iota(jnp.int32, (TILE, targets.shape[1]), 0)).astype(BF16)


def ring_targets():
    node = lax.axis_index("node")
    position = lax.rem(node, RING)
    plane = node - position
    after = plane + lax.rem(position + 1, RING)
    before = plane + lax.rem(position + RING - 1, RING)
    across = lax.rem(node + RING, 2 * RING)
    return node, position, (after, before, across)


def sum_chunk(k, first_row, slots_s, edges_v, head_ref, query_ref, win_ref, rel_ref, message_ref, mixed_ref):
    slot_total = edges_v.shape[2]

    def tile_step(j):
        tile = 2 * k + j

        def block(b):
            base = slot_base(tile, b)
            for u in range(UNROLL):
                place = pl.multiple_of((b * UNROLL + u) * 4, 4)
                message_ref[pl.ds(place, 4), :] = win_ref[slots_s[base + u]]

        each(slot_total // UNROLL, block)
        onehot = target_onehot(edges_v, tile)
        row = pl.multiple_of(j * TILE, TILE)
        ids = first_row + tile * TILE + lax.broadcasted_iota(jnp.int32, (TILE, LANES), 0)
        scale = rel_ref[pl.ds(pl.multiple_of(tile * slot_total, slot_total), slot_total), :]
        for half in range(2):
            message = jnp.concatenate(
                [
                    (message_ref[pl.ds(2 * half + c, slot_total, stride=4), :] * scale).astype(BF16)
                    for c in range(2)
                ],
                axis=1,
            )
            summed = jnp.dot(onehot, message, preferred_element_type=F32)
            for c in range(2):
                cols = slice((2 * half + c) * LANES, (2 * half + c + 1) * LANES)
                start = jnp.where(ids == head_ref[:, cols], query_ref[:, cols], 0.0)
                mixed_ref[pl.ds(row, TILE), cols] = start + summed[:, c * LANES : (c + 1) * LANES]

    each(2, tile_step)


def forward_kernel(
    state_hbm, cot_hbm, slots_s, head_s, chosen_s, edges_v, table_t, rel_t, weight_ref, bias_ref,
    state_out, grad_out, mixed_out, slope_out, sums_out,
    own, middle, mixed_own, cot, inbox, win_a, win_b, rel_a, rel_b, padded, table_ref, message_ref, mixed_ref,
    wide_ref, head_ref, query_ref, copy_sem, send_sem, recv_sem,
):
    node, position, targets = ring_targets()
    rows = own.shape[0]
    barrier = pltpu.get_barrier_semaphore()
    for target in targets:
        pl.semaphore_signal(barrier, inc=1, device_id={"node": target}, device_id_type=MESH)
    own_copy = pltpu.make_async_copy(state_hbm, own, copy_sem.at[0])
    cot_copy = pltpu.make_async_copy(cot_hbm, cot, copy_sem.at[1])
    own_copy.start()
    cot_copy.start()
    pl.semaphore_wait(barrier, 3)

    def piece(trip, way, k, source):
        return pltpu.make_async_remote_copy(
            src_ref=source.at[chunk_rows(k), :],
            dst_ref=inbox.at[trip, way, chunk_rows(k), :],
            send_sem=send_sem.at[trip, way, k],
            recv_sem=recv_sem.at[trip, way, k],
            device_id={"node": targets[way]},
            device_id_type=MESH,
        )

    def send_chunk(trip, k, source):
        piece(trip, 2, k, source).start()

        @pl.when(position != RING - 1)
        def _():
            piece(trip, 0, k, source).start()

        @pl.when(position != 0)
        def _():
            piece(trip, 1, k, source).start()

    def relay_chunk(trip, k):
        mirrored = inbox.at[trip, 2]
        piece(trip, 2, k, mirrored).wait_recv()

        @pl.when(position == RING - 1)
        def _():
            piece(trip, 0, k, mirrored).start()

        @pl.when(position == 0)
        def _():
            piece(trip, 1, k, mirrored).start()

    def fill(win, quarter, k, block):
        spread_rows(win, quarter * rows + k * CHUNK, block.astype(F32))

    each(CHUNKS, lambda k: send_chunk(0, k, state_hbm))

    spread_table(table_ref, table_t)
    for layer, target in enumerate((rel_a, rel_b)):
        pad_columns(padded, rel_t.at[layer])
        relation_rows(target, padded, edges_v)
    lane = lax.broadcasted_iota(jnp.int32, (1, LANES), 1) // DIM
    for c in range(4):
        heads = jnp.zeros((1, LANES), jnp.int32)
        vectors = jnp.zeros((1, LANES), F32)
        for k in range(4):
            heads = jnp.where(lane == k, head_s[4 * c + k], heads)
            vectors = jnp.where(lane == k, table_ref[chosen_s[4 * c + k]][0:1], vectors)
        head_ref[:, c * LANES : (c + 1) * LANES] = heads
        query_ref[:, c * LANES : (c + 1) * LANES] = vectors.astype(BF16).astype(F32)
    for layer in range(2):
        high, low = split_pair(block_diagonal(weight_ref[layer]))
        wide_ref[2 * layer] = high
        wide_ref[2 * layer + 1] = low
    bias_zero = jnp.concatenate([bias_ref[0:1, :]] * 8, axis=1)
    bias_one = jnp.concatenate([bias_ref[1:2, :]] * 8, axis=1)
    first_row = node * rows

    own_copy.wait()
    each(CHUNKS, lambda k: fill(win_a, 1, k, own[chunk_rows(k), :]))

    def take_first_mirror(k):
        relay_chunk(0, k)
        fill(win_a, 3, k, inbox[0, 2, chunk_rows(k), :])

    def take_first_sides(k):
        for way, quarter in ((0, 0), (1, 2)):
            piece(0, way, k, own).wait_recv()
            fill(win_a, quarter, k, inbox[0, way, chunk_rows(k), :])

    each(CHUNKS, take_first_mirror)
    each(CHUNKS, take_first_sides)

    def next_state(state, update, quarter, k, half):
        sigma = jax.nn.sigmoid(update)
        place = pl.ds(pl.multiple_of(quarter * rows + k * CHUNK, CHUNK), CHUNK)
        slope_out[place, half * 256 : half * 256 + 256] = (sigma * (1.0 + update * (1.0 - sigma))).astype(BF16)
        result = (state.astype(F32) + update * sigma).astype(BF16)
        for c in range(2):
            flat(win_b)[pl.ds((quarter * rows + k * CHUNK) * 4 + half * 2 + c, CHUNK, stride=4), :] = result[
                :, c * LANES : (c + 1) * LANES
            ].astype(F32)
        return result

    def remote_state(way, quarter, k):
        at = chunk_rows(k)
        place = pl.ds(pl.multiple_of(quarter * rows + k * CHUNK, CHUNK), CHUNK)
        for half in range(2):
            cols = slice(half * 256, half * 256 + 256)
            mixed = inbox[1, way, at, cols]
            mixed_out[place, cols] = mixed
            update = half_dot(mixed, wide_ref[0], 0) + half_dot(mixed, wide_ref[1], 0) + bias_zero
            next_state(inbox[0, way, at, cols], update, quarter, k, half)

    def take_second_mirror(k):
        relay_chunk(1, k)
        remote_state(2, 3, k)

    def take_second_sides(k):
        for way, quarter in ((0, 0), (1, 2)):
            piece(1, way, k, own).wait_recv()
            remote_state(way, quarter, k)

    def zero_step(k):
        sum_chunk(k, first_row, slots_s, edges_v, head_ref, query_ref, win_a, rel_a, message_ref, mixed_ref)
        at = chunk_rows(k)
        mixed_own[at, :] = mixed_ref[...].astype(BF16)
        send_chunk(1, k, mixed_own)
        for half in range(2):
            cols = slice(half * 256, half * 256 + 256)
            update = split_dot(mixed_ref[:, cols], wide_ref[0], wide_ref[1]) + bias_zero
            middle[at, cols] = next_state(own[at, cols], update, 1, k, half)
        mixed_out[pl.ds(pl.multiple_of(rows + k * CHUNK, CHUNK), CHUNK), :] = mixed_own[at, :]

        @pl.when(k >= 3)
        def _():
            take_second_mirror(k - 3)

        @pl.when(k >= 5)
        def _():
            take_second_sides(k - 5)

    each(CHUNKS, zero_step)
    each(3, lambda k: take_second_mirror(k + CHUNKS - 3))
    each(5, lambda k: take_second_sides(k + CHUNKS - 5))
    cot_copy.wait()

    def one_step(k, carry):
        product, bias_sum = carry
        sum_chunk(k, first_row, slots_s, edges_v, head_ref, query_ref, win_b, rel_b, message_ref, mixed_ref)
        at = chunk_rows(k)
        for half in range(2):
            cols = slice(half * 256, half * 256 + 256)
            mixed = mixed_ref[:, cols]
            update = split_dot(mixed, wide_ref[2], wide_ref[3]) + bias_one
            sigma = jax.nn.sigmoid(update)
            state_out[at, cols] = (middle[at, cols].astype(F32) + update * sigma).astype(BF16)
            grad = cot[at, cols].astype(F32) * (sigma * (1.0 + update * (1.0 - sigma)))
            grad_out[at, cols] = split_dot(grad, wide_ref[2], wide_ref[3], 1).astype(BF16)
            for c in range(2):
                part = slice(c * LANES, (c + 1) * LANES)
                product += product_of(mixed[:, part].astype(BF16), grad[:, part].astype(BF16))
                bias_sum += jnp.sum(grad[:, part], axis=0, keepdims=True)
        return product, bias_sum

    product, bias_sum = lax.fori_loop(
        0, CHUNKS, one_step, (jnp.zeros((LANES, LANES), F32), jnp.zeros((1, LANES), F32))
    )
    sums_out[0:8, :] = block_sums(product)
    sums_out[8:16, :] = fold_lanes(jnp.broadcast_to(bias_sum, (8, LANES)))
    for trip in range(2):
        for way in range(3):
            each(CHUNKS, lambda k: piece(trip, way, k, own).wait_send())


def scatter_kernel(
    state_in, slots_s, edges_v, grad_ref, rel_t, mixed_ref, slope_ref, cot_ref, sums_in, state_out, sums_out,
    first_ref, second_ref, rel_ref, padded, term_ref, copy_sem,
):
    state_copy = pltpu.make_async_copy(state_in, state_out, copy_sem)
    state_copy.start()
    rows = cot_ref.shape[0]
    tiles, slot_total = edges_v.shape[1:]
    pad_columns(padded, rel_t.at[1])
    relation_rows(rel_ref, padded, edges_v)
    flat_first, flat_second = flat(first_ref), flat(second_ref)

    def clear(i):
        at = pl.ds(pl.multiple_of(i * 256, 256), 256)
        flat_first[at, :] = jnp.zeros((256, LANES), F32)
        flat_second[at, :] = jnp.zeros((256, LANES), F32)

    each(rows * 16 // 256, clear)

    def tile_step(tile):
        onehot = target_onehot(edges_v, tile)
        scale = rel_ref[pl.ds(pl.multiple_of(tile * slot_total, slot_total), slot_total), :]
        grads = grad_ref[pl.ds(pl.multiple_of(tile * TILE, TILE), TILE), :]
        for half in range(2):
            picked = product_of(onehot, grads[:, half * 256 : half * 256 + 256])
            for c in range(2):
                term_ref[pl.ds(2 * half + c, slot_total, stride=4), :] = picked[:, c * LANES : (c + 1) * LANES] * scale

        def block(b):
            base = slot_base(tile, b)
            for u in range(UNROLL):
                total = first_ref if u % 2 == 0 else second_ref
                slot = slots_s[base + u]
                place = pl.multiple_of((b * UNROLL + u) * 4, 4)
                total[slot] = total[slot] + term_ref[pl.ds(place, 4), :]

        each(slot_total // UNROLL, block)

    each(tiles, tile_step)

    def collect(i, carry):
        product, bias_sum = carry
        start = pl.multiple_of(i * CHUNK, CHUNK)
        at = pl.ds(start, CHUNK)
        own_rows = pl.ds(pl.multiple_of(lax.rem(i, CHUNKS) * CHUNK, CHUNK), CHUNK)
        mine = i // CHUNKS == 1
        for c in range(4):
            cols = slice(c * LANES, (c + 1) * LANES)
            place = pl.ds(start * 4 + c, CHUNK, stride=4)
            terms = flat_first[place, :] + flat_second[place, :]
            terms += jnp.where(mine, cot_ref[own_rows, cols].astype(F32), 0.0)
            grad = terms * slope_ref[at, cols].astype(F32)
            product += product_of(mixed_ref[at, cols], grad.astype(BF16))
            bias_sum += jnp.sum(grad, axis=0, keepdims=True)
        return product, bias_sum

    product, bias_sum = lax.fori_loop(
        0, 4 * CHUNKS, collect, (jnp.zeros((LANES, LANES), F32), jnp.zeros((1, LANES), F32))
    )
    sums_out[0:8, :] = block_sums(product)
    sums_out[8:16, :] = sums_in[0:8, :]
    sub = lax.broadcasted_iota(jnp.int32, (8, LANES), 0)
    sums_out[16:24, :] = jnp.where(sub == 0, fold_lanes(jnp.broadcast_to(bias_sum, (8, LANES))), sums_in[8:16, :])
    state_copy.wait()


def total_kernel(
    sums_ref, weight_out, bias_out, mine, first_buf, second_buf, first_send, first_recv, second_send, second_recv
):
    node = lax.axis_index("node")
    query = lax.axis_index("query")
    position = lax.rem(node, RING)
    half = node // RING
    in_first = half * 4 + query
    barrier = pltpu.get_barrier_semaphore()

    def first_peer(j):
        return {"node": (j // 4) * RING + position, "query": lax.rem(j, 4)}

    def second_peer(j):
        return {"node": half * RING + j, "query": query}

    for d in range(1, 8):
        pl.semaphore_signal(barrier, inc=1, device_id=first_peer(lax.rem(in_first + d, 8)), device_id_type=MESH)
    for d in range(1, RING):
        pl.semaphore_signal(barrier, inc=1, device_id=second_peer(lax.rem(position + d, RING)), device_id_type=MESH)
    pl.semaphore_wait(barrier, 22)

    def stage(source, buf, send, recv, me, peer, count):
        def piece(slot, to):
            return pltpu.make_async_remote_copy(
                src_ref=source, dst_ref=buf.at[slot], send_sem=send.at[to], recv_sem=recv.at[slot],
                device_id=peer(to), device_id_type=MESH,
            )

        others = [lax.rem(me + d, count) for d in range(1, count)]
        for to in others:
            piece(me, to).start()
        buf[me] = source[...]
        for other in others:
            piece(other, other).wait_recv()
        total = buf[0]
        for j in range(1, count):
            total = total + buf[j]
        return total, lambda: [piece(me, to).wait_send() for to in others]

    total, finish_first = stage(sums_ref, first_buf, first_send, first_recv, in_first, first_peer, 8)
    mine[...] = total
    total, finish_second = stage(mine, second_buf, second_send, second_recv, position, second_peer, RING)
    for l in range(2):
        packed = total[8 * l : 8 * l + 8, :]
        for k in range(4):
            moved = packed if k == 0 else pltpu.roll(packed, LANES - 32 * k, 1)
            weight_out[l, 8 * k : 8 * k + 8, :] = moved[:, 0:32]
    bias_out[...] = total[16:18, 0:32]
    finish_first()
    finish_second()


def body(
    entity_state, edge_tiles, query_head, query_relation, query_table, rel_vectors, mix_weight, mix_bias, cotangent
):
    rows, cols = entity_state.shape
    tiles, unused, slot_total = edge_tiles.shape
    edge_count = tiles * slot_total
    rel_rows = rel_vectors.shape[1]
    padded_rows = -(-rel_rows // LANES) * LANES
    edges = edge_tiles.transpose(1, 0, 2)
    slots = edges.reshape(3, tiles // 8, 8, slot_total // LANES, LANES).transpose(0, 1, 3, 2, 4).reshape(3 * edge_count)
    table_t = query_table.T
    rel_t = rel_vectors.transpose(0, 2, 1)
    smem = pl.BlockSpec(memory_space=pltpu.SMEM)
    vmem = pl.BlockSpec(memory_space=pltpu.VMEM)
    anywhere = pl.BlockSpec(memory_space=pl.ANY)
    half = jax.ShapeDtypeStruct((rows, cols), BF16)
    wide = jax.ShapeDtypeStruct((4 * rows, cols), BF16)
    packet = (24, LANES)
    block = pltpu.VMEM((rows, cols), BF16)
    window = pltpu.VMEM((rows * 4, 4, LANES), F32)
    edge_rows = pltpu.VMEM((edge_count, LANES), F32)
    padded = pltpu.VMEM((DIM, padded_rows), F32)
    message = pltpu.VMEM((slot_total * 4, LANES), F32)
    state_two, grad_mixed, mixed_zero, slope_zero, sums = pl.pallas_call(
        forward_kernel,
        out_shape=(half, half, wide, wide, jax.ShapeDtypeStruct((16, LANES), F32)),
        in_specs=[anywhere] * 2 + [smem] * 3 + [vmem] * 5,
        out_specs=(vmem,) * 5,
        scratch_shapes=[
            block,
            block,
            block,
            block,
            pltpu.VMEM((2, 3, rows, cols), BF16),
            window,
            window,
            edge_rows,
            edge_rows,
            padded,
            pltpu.VMEM((rel_rows, 4, LANES), F32),
            message,
            pltpu.VMEM((CHUNK, cols), F32),
            pltpu.VMEM((4, 256, 256), BF16),
            pltpu.VMEM((1, cols), jnp.int32),
            pltpu.VMEM((1, cols), F32),
            pltpu.SemaphoreType.DMA((2,)),
            pltpu.SemaphoreType.DMA((2, 3, CHUNKS)),
            pltpu.SemaphoreType.DMA((2, 3, CHUNKS)),
        ],
        compiler_params=pltpu.CompilerParams(
            vmem_limit_bytes=VMEM_BYTES, collective_id=0, has_side_effects=True
        ),
        name="two_layers",
    )(
        entity_state, cotangent, slots, query_head, query_relation, edges, table_t, rel_t, mix_weight, mix_bias
    )
    state_out, sums = pl.pallas_call(
        scatter_kernel,
        out_shape=(half, jax.ShapeDtypeStruct(packet, F32)),
        in_specs=[anywhere, smem] + [vmem] * 7,
        out_specs=(anywhere, vmem),
        scratch_shapes=[window, window, edge_rows, padded, message, pltpu.SemaphoreType.DMA],
        compiler_params=pltpu.CompilerParams(vmem_limit_bytes=VMEM_BYTES),
        name="scatter_terms",
    )(state_two, slots, edges, grad_mixed, rel_t, mixed_zero, slope_zero, cotangent, sums)
    weight_grads, bias_grads = pl.pallas_call(
        total_kernel,
        out_shape=(jax.ShapeDtypeStruct((2, DIM, DIM), F32), jax.ShapeDtypeStruct((2, DIM), F32)),
        in_specs=[vmem],
        out_specs=(vmem,) * 2,
        scratch_shapes=[
            pltpu.VMEM(packet, F32),
            pltpu.VMEM((8,) + packet, F32),
            pltpu.VMEM((RING,) + packet, F32),
            pltpu.SemaphoreType.DMA((8,)),
            pltpu.SemaphoreType.DMA((8,)),
            pltpu.SemaphoreType.DMA((RING,)),
            pltpu.SemaphoreType.DMA((RING,)),
        ],
        compiler_params=pltpu.CompilerParams(collective_id=1, has_side_effects=True),
        name="total_sums",
    )(sums)
    return state_out, weight_grads, bias_grads


def solution(mesh):
    placed = (
        P("node", "query"),
        P("node", None, None),
        P("query"),
        P("query"),
        P(),
        P(),
        P(),
        P(),
        P("node", "query"),
    )
    return jax.shard_map(
        body, mesh=mesh, in_specs=placed, out_specs=(P("node", "query"), P(), P()), check_vma=False
    )
```

time: 251 us -> 179 us (0.71)
  Pallas kernels: 247 us -> 176 us
    pallas_call x3, Pallas kernels: 247 us -> 176 us  [the longest x1 112 us: body(): pl.pallas_call(forward_kernel, out_shape=(half, half, wide, wide, jax.Sha...]
where the time goes in v3:
time: 179 us
  Pallas kernels  176 us (98%)
  local copies, waits for them, and re-layouts  2.57 us (1%)
    pallas_call x1, Pallas kernels, body(): pl.pallas_call(forward_kernel, out_shape=(half, half, wide, wide, jax.Sha...  112 us
    pallas_call x1, Pallas kernels, body(): pl.pallas_call(scatter_kernel, out_shape=(half, jax.ShapeDtypeStruct(pack...  48.5 us
    pallas_call x1, Pallas kernels, body(): pl.pallas_call(total_kernel, out_shape=(jax.ShapeDtypeStruct((2, DIM, DIM...  15.2 us

profile of v3, /device:TPU:0, one launch (start us, length us, event | category | flops | bytes accessed | tf_op | source)
XLA Modules:
  0.0 178.9 jit_solution(12203490897117538960)
XLA Ops:
  0.6 112.0 %two_layers.1 = (bf16[1024,512]{1,0:T(8,128)(2,1)}, bf16[1024,512]{1,0:T(8,128)(2,1)}, bf16[4096,512]{1,0:T(8,128)(2,1)}, bf16[4096,512]{1,0:T(8,128)(2,1)}, f32[16,128]{1,0:T(8,128)}) custom-call(bf16[1024,512]{1,0:T(8,128)(2,1)} %state_hbm.1, bf16[1024,512]{1,0:T(8,128)(2,1)} %cot_ref.1, s32[24576]{0:T(1024)} %bitcast.9, s32[16]{0:T(128)} %head_s.1, ...), custom_call_target="tpu_custom_call" | custom-call | tf_op jit(solution)/shard_map/two_layers/pallas_call | solution.py:492
  112.7 48.5 %scatter_terms.1 = (bf16[1024,512]{1,0:T(8,128)(2,1)}, f32[24,128]{1,0:T(8,128)}) custom-call(bf16[1024,512]{1,0:T(8,128)(2,1)} %get-tuple-element.12.state_in, s32[24576]{0:T(1024)} %bitcast.11, s32[3,16,512]{2,1,0:T(8,128)} %bitcast.12, bf16[1024,512]{1,0:T(8,128)(2,1)} %get-tuple-element.13.grad_ref, f32[2,32,822]{2,1,0:T(8,128)} %bitcast.14, ...), custom_call_target="tpu_custom_call" | custom-call | tf_op jit(solution)/shard_map/scatter_terms/pallas_call | solution.py:525
  161.1 15.2 %total_sums.1 = (f32[2,32,32]{2,1,0:T(8,128)}, f32[2,32]{1,0:T(2,128)}) custom-call(f32[24,128]{1,0:T(8,128)} %get-tuple-element.18.sums_ref), custom_call_target="tpu_custom_call" | custom-call | tf_op jit(solution)/shard_map/total_sums/pallas_call | solution.py:534
  176.3 1.4 copy.14
  177.7 1.2 copy.15

commit v4 on v3

--- a/solution.py
+++ b/solution.py
@@ -11,7 +11,8 @@
 CHUNK = 128
 CHUNKS = 8
 RING = 16
-UNROLL = 32
+WINDOW = 3
+SUMS = 4
 F32 = jnp.float32
 BF16 = jnp.bfloat16
 MESH = pl.DeviceIdType.MESH
@@ -121,8 +122,12 @@
     return pl.ds(pl.multiple_of(k * CHUNK, CHUNK), CHUNK)
 
 
-def slot_base(tile, block):
-    return (tile // 8 * 4 + block // 4) * 1024 + lax.rem(tile, 8) * LANES + lax.rem(block, 4) * UNROLL
+def slot_base(tile):
+    return tile // 8 * 4096 + lax.rem(tile, 8) * LANES
+
+
+def slot_step(edge):
+    return edge // LANES * 1024 + edge % LANES
 
 
 def target_onehot(edges_v, tile):
@@ -146,41 +151,33 @@
     def tile_step(j):
         tile = 2 * k + j
 
-        def block(b):
-            base = slot_base(tile, b)
-            for u in range(UNROLL):
-                place = pl.multiple_of((b * UNROLL + u) * 4, 4)
-                message_ref[pl.ds(place, 4), :] = win_ref[slots_s[base + u]]
-
-        each(slot_total // UNROLL, block)
+        base = slot_base(tile)
+        for edge in range(slot_total):
+            message_ref[4 * edge : 4 * edge + 4, :] = win_ref[slots_s[base + slot_step(edge)]]
         onehot = target_onehot(edges_v, tile)
         row = pl.multiple_of(j * TILE, TILE)
         ids = first_row + tile * TILE + lax.broadcasted_iota(jnp.int32, (TILE, LANES), 0)
         scale = rel_ref[pl.ds(pl.multiple_of(tile * slot_total, slot_total), slot_total), :]
-        for half in range(2):
-            message = jnp.concatenate(
-                [
-                    (message_ref[pl.ds(2 * half + c, slot_total, stride=4), :] * scale).astype(BF16)
-                    for c in range(2)
-                ],
-                axis=1,
-            )
-            summed = jnp.dot(onehot, message, preferred_element_type=F32)
-            for c in range(2):
-                cols = slice((2 * half + c) * LANES, (2 * half + c + 1) * LANES)
-                start = jnp.where(ids == head_ref[:, cols], query_ref[:, cols], 0.0)
-                mixed_ref[pl.ds(row, TILE), cols] = start + summed[:, c * LANES : (c + 1) * LANES]
+        message = jnp.concatenate(
+            [(message_ref[pl.ds(c, slot_total, stride=4), :] * scale).astype(BF16) for c in range(4)], axis=1
+        )
+        summed = jnp.dot(onehot, message, preferred_element_type=F32)
+        for c in range(4):
+            cols = slice(c * LANES, (c + 1) * LANES)
+            start = jnp.where(ids == head_ref[:, cols], query_ref[:, cols], 0.0)
+            mixed_ref[pl.ds(row, TILE), cols] = start + summed[:, cols]
 
     each(2, tile_step)
 
 
 def forward_kernel(
     state_hbm, cot_hbm, slots_s, head_s, chosen_s, edges_v, table_t, rel_t, weight_ref, bias_ref,
-    state_out, grad_out, mixed_out, slope_out, sums_out,
-    own, middle, mixed_own, cot, inbox, win_a, win_b, rel_a, rel_b, padded, table_ref, message_ref, mixed_ref,
-    wide_ref, head_ref, query_ref, copy_sem, send_sem, recv_sem,
+    state_out, grad_out, mixed_out, slope_out, rel_out, sums_out, places_out,
+    own, middle, mixed_own, cot, state_ref, grad_ref, slope_ref, inbox, win_a, win_b, rel_a, rel_b, padded, table_ref,
+    message_ref, mixed_ref, wide_ref, head_ref, query_ref, copy_sem, send_sem, recv_sem,
 ):
     node, position, targets = ring_targets()
+    at_end = jnp.logical_or(position == 0, position == RING - 1)
     rows = own.shape[0]
     barrier = pltpu.get_barrier_semaphore()
     for target in targets:
@@ -201,9 +198,7 @@
             device_id_type=MESH,
         )
 
-    def send_chunk(trip, k, source):
-        piece(trip, 2, k, source).start()
-
+    def send_sides(trip, k, source):
         @pl.when(position != RING - 1)
         def _():
             piece(trip, 0, k, source).start()
@@ -227,12 +222,22 @@
     def fill(win, quarter, k, block):
         spread_rows(win, quarter * rows + k * CHUNK, block.astype(F32))
 
-    each(CHUNKS, lambda k: send_chunk(0, k, state_hbm))
+    def start_first(k):
+        send_sides(0, k, state_hbm)
+
+        @pl.when(jnp.logical_or(jnp.logical_not(at_end), k < WINDOW))
+        def _():
+            piece(0, 2, k, state_hbm).start()
+
+    each(CHUNKS, start_first)
 
     spread_table(table_ref, table_t)
     for layer, target in enumerate((rel_a, rel_b)):
         pad_columns(padded, rel_t.at[layer])
         relation_rows(target, padded, edges_v)
+    rel_copy = pltpu.make_async_copy(rel_b, rel_out, copy_sem.at[2])
+    rel_copy.start()
+    places_out[...] = edges_v[0] * 4
     lane = lax.broadcasted_iota(jnp.int32, (1, LANES), 1) // DIM
     for c in range(4):
         heads = jnp.zeros((1, LANES), jnp.int32)
@@ -255,6 +260,11 @@
 
     def take_first_mirror(k):
         relay_chunk(0, k)
+
+        @pl.when(jnp.logical_and(at_end, k + WINDOW < CHUNKS))
+        def _():
+            piece(0, 2, k + WINDOW, state_hbm).start()
+
         fill(win_a, 3, k, inbox[0, 2, chunk_rows(k), :])
 
     def take_first_sides(k):
@@ -268,7 +278,7 @@
     def next_state(state, update, quarter, k, half):
         sigma = jax.nn.sigmoid(update)
         place = pl.ds(pl.multiple_of(quarter * rows + k * CHUNK, CHUNK), CHUNK)
-        slope_out[place, half * 256 : half * 256 + 256] = (sigma * (1.0 + update * (1.0 - sigma))).astype(BF16)
+        slope_ref[place, half * 256 : half * 256 + 256] = (sigma * (1.0 + update * (1.0 - sigma))).astype(BF16)
         result = (state.astype(F32) + update * sigma).astype(BF16)
         for c in range(2):
             flat(win_b)[pl.ds((quarter * rows + k * CHUNK) * 4 + half * 2 + c, CHUNK, stride=4), :] = result[
@@ -278,11 +288,9 @@
 
     def remote_state(way, quarter, k):
         at = chunk_rows(k)
-        place = pl.ds(pl.multiple_of(quarter * rows + k * CHUNK, CHUNK), CHUNK)
         for half in range(2):
             cols = slice(half * 256, half * 256 + 256)
             mixed = inbox[1, way, at, cols]
-            mixed_out[place, cols] = mixed
             update = half_dot(mixed, wide_ref[0], 0) + half_dot(mixed, wide_ref[1], 0) + bias_zero
             next_state(inbox[0, way, at, cols], update, quarter, k, half)
 
@@ -299,13 +307,12 @@
         sum_chunk(k, first_row, slots_s, edges_v, head_ref, query_ref, win_a, rel_a, message_ref, mixed_ref)
         at = chunk_rows(k)
         mixed_own[at, :] = mixed_ref[...].astype(BF16)
-        send_chunk(1, k, mixed_own)
+        piece(1, 2, k, mixed_own).start()
+        send_sides(1, k, mixed_own)
         for half in range(2):
             cols = slice(half * 256, half * 256 + 256)
             update = split_dot(mixed_ref[:, cols], wide_ref[0], wide_ref[1]) + bias_zero
             middle[at, cols] = next_state(own[at, cols], update, 1, k, half)
-        mixed_out[pl.ds(pl.multiple_of(rows + k * CHUNK, CHUNK), CHUNK), :] = mixed_own[at, :]
-
         @pl.when(k >= 3)
         def _():
             take_second_mirror(k - 3)
@@ -318,6 +325,20 @@
     each(3, lambda k: take_second_mirror(k + CHUNKS - 3))
     each(5, lambda k: take_second_sides(k + CHUNKS - 5))
     cot_copy.wait()
+    window_copies = [pltpu.make_async_copy(slope_ref, slope_out, copy_sem.at[3])]
+    for quarter, source in enumerate((inbox.at[1, 0], mixed_own, inbox.at[1, 1], inbox.at[1, 2])):
+        window_copies.append(
+            pltpu.make_async_copy(source, mixed_out.at[pl.ds(quarter * rows, rows), :], copy_sem.at[4 + quarter])
+        )
+    for copy in window_copies:
+        copy.start()
+
+    def result_copies(k):
+        at = chunk_rows(k)
+        return (
+            pltpu.make_async_copy(state_ref.at[at, :], state_out.at[at, :], copy_sem.at[8 + 2 * k]),
+            pltpu.make_async_copy(grad_ref.at[at, :], grad_out.at[at, :], copy_sem.at[9 + 2 * k]),
+        )
 
     def one_step(k, carry):
         product, bias_sum = carry
@@ -328,13 +349,15 @@
             mixed = mixed_ref[:, cols]
             update = split_dot(mixed, wide_ref[2], wide_ref[3]) + bias_one
             sigma = jax.nn.sigmoid(update)
-            state_out[at, cols] = (middle[at, cols].astype(F32) + update * sigma).astype(BF16)
+            state_ref[at, cols] = (middle[at, cols].astype(F32) + update * sigma).astype(BF16)
             grad = cot[at, cols].astype(F32) * (sigma * (1.0 + update * (1.0 - sigma)))
-            grad_out[at, cols] = split_dot(grad, wide_ref[2], wide_ref[3], 1).astype(BF16)
+            grad_ref[at, cols] = split_dot(grad, wide_ref[2], wide_ref[3], 1).astype(BF16)
             for c in range(2):
                 part = slice(c * LANES, (c + 1) * LANES)
                 product += product_of(mixed[:, part].astype(BF16), grad[:, part].astype(BF16))
                 bias_sum += jnp.sum(grad[:, part], axis=0, keepdims=True)
+        for copy in result_copies(k):
+            copy.start()
         return product, bias_sum
 
     product, bias_sum = lax.fori_loop(
@@ -345,47 +368,64 @@
     for trip in range(2):
         for way in range(3):
             each(CHUNKS, lambda k: piece(trip, way, k, own).wait_send())
+    rel_copy.wait()
+    for copy in window_copies:
+        copy.wait()
+    each(CHUNKS, lambda k: [copy.wait() for copy in result_copies(k)])
 
 
 def scatter_kernel(
-    state_in, slots_s, edges_v, grad_ref, rel_t, mixed_ref, slope_ref, cot_ref, sums_in, state_out, sums_out,
-    first_ref, second_ref, rel_ref, padded, term_ref, copy_sem,
+    state_in, mixed_in, slope_in, rel_in, places_s, edges_v, grad_ref, cot_ref, sums_in, state_out, sums_out,
+    first_ref, second_ref, third_ref, fourth_ref, rel_ref, mixed_ref, slope_ref, term_ref, copy_sem,
 ):
-    state_copy = pltpu.make_async_copy(state_in, state_out, copy_sem)
-    state_copy.start()
-    rows = cot_ref.shape[0]
+    copies = [
+        pltpu.make_async_copy(source, target, copy_sem.at[i])
+        for i, (source, target) in enumerate(
+            ((rel_in, rel_ref), (state_in, state_out), (mixed_in, mixed_ref), (slope_in, slope_ref))
+        )
+    ]
+    for copy in copies:
+        copy.start()
+    totals = (first_ref, second_ref, third_ref, fourth_ref)
     tiles, slot_total = edges_v.shape[1:]
-    pad_columns(padded, rel_t.at[1])
-    relation_rows(rel_ref, padded, edges_v)
-    flat_first, flat_second = flat(first_ref), flat(second_ref)
+    half_total = slot_total // 2
 
     def clear(i):
         at = pl.ds(pl.multiple_of(i * 256, 256), 256)
-        flat_first[at, :] = jnp.zeros((256, LANES), F32)
-        flat_second[at, :] = jnp.zeros((256, LANES), F32)
-
-    each(rows * 16 // 256, clear)
+        for total in totals:
+            total[at, :] = jnp.zeros((256, LANES), F32)
+
+    each(first_ref.shape[0] // 256, clear)
+    copies[0].wait()
+
+    def make_terms(tile, half):
+        edges = slice(half * half_total, half * half_total + half_total)
+        onehot = target_onehot(edges_v, tile)[:, edges]
+        start = pl.multiple_of(tile * slot_total + half * half_total, half_total)
+        scale = rel_ref[pl.ds(start, half_total), :]
+        picked = product_of(onehot, grad_ref[pl.ds(pl.multiple_of(tile * TILE, TILE), TILE), :])
+        for c in range(4):
+            place = pl.ds(4 * half * half_total + c, half_total, stride=4)
+            term_ref[place, :] = picked[:, c * LANES : (c + 1) * LANES] * scale
+
+    def add_terms(tile, half):
+        base = slot_base(tile)
+        for edge in range(half * half_total, (half + 1) * half_total):
+            total = totals[edge % SUMS]
+            place = pl.ds(pl.multiple_of(places_s[base + slot_step(edge)], 4), 4)
+            total[place, :] = total[place, :] + term_ref[4 * edge : 4 * edge + 4, :]
+
+    make_terms(0, 0)
 
     def tile_step(tile):
-        onehot = target_onehot(edges_v, tile)
-        scale = rel_ref[pl.ds(pl.multiple_of(tile * slot_total, slot_total), slot_total), :]
-        grads = grad_ref[pl.ds(pl.multiple_of(tile * TILE, TILE), TILE), :]
-        for half in range(2):
-            picked = product_of(onehot, grads[:, half * 256 : half * 256 + 256])
-            for c in range(2):
-                term_ref[pl.ds(2 * half + c, slot_total, stride=4), :] = picked[:, c * LANES : (c + 1) * LANES] * scale
-
-        def block(b):
-            base = slot_base(tile, b)
-            for u in range(UNROLL):
-                total = first_ref if u % 2 == 0 else second_ref
-                slot = slots_s[base + u]
-                place = pl.multiple_of((b * UNROLL + u) * 4, 4)
-                total[slot] = total[slot] + term_ref[pl.ds(place, 4), :]
-
-        each(slot_total // UNROLL, block)
+        add_terms(tile, 0)
+        make_terms(tile, 1)
+        add_terms(tile, 1)
+        make_terms(jnp.minimum(tile + 1, tiles - 1), 0)
 
     each(tiles, tile_step)
+    for copy in copies[1:]:
+        copy.wait()
 
     def collect(i, carry):
         product, bias_sum = carry
@@ -396,7 +436,7 @@
         for c in range(4):
             cols = slice(c * LANES, (c + 1) * LANES)
             place = pl.ds(start * 4 + c, CHUNK, stride=4)
-            terms = flat_first[place, :] + flat_second[place, :]
+            terms = (first_ref[place, :] + second_ref[place, :]) + (third_ref[place, :] + fourth_ref[place, :])
             terms += jnp.where(mine, cot_ref[own_rows, cols].astype(F32), 0.0)
             grad = terms * slope_ref[at, cols].astype(F32)
             product += product_of(mixed_ref[at, cols], grad.astype(BF16))
@@ -410,7 +450,6 @@
     sums_out[8:16, :] = sums_in[0:8, :]
     sub = lax.broadcasted_iota(jnp.int32, (8, LANES), 0)
     sums_out[16:24, :] = jnp.where(sub == 0, fold_lanes(jnp.broadcast_to(bias_sum, (8, LANES))), sums_in[8:16, :])
-    state_copy.wait()
 
 
 def total_kernel(
@@ -466,6 +505,11 @@
     finish_second()
 
 
+def in_memory_order(table):
+    cols = table.shape[-1]
+    return table.reshape(-1, 8, cols // LANES, LANES).transpose(0, 2, 1, 3).reshape(table.size)
+
+
 def body(
     entity_state, edge_tiles, query_head, query_relation, query_table, rel_vectors, mix_weight, mix_bias, cotangent
 ):
@@ -475,7 +519,7 @@
     rel_rows = rel_vectors.shape[1]
     padded_rows = -(-rel_rows // LANES) * LANES
     edges = edge_tiles.transpose(1, 0, 2)
-    slots = edges.reshape(3, tiles // 8, 8, slot_total // LANES, LANES).transpose(0, 1, 3, 2, 4).reshape(3 * edge_count)
+    slots = in_memory_order(edges)
     table_t = query_table.T
     rel_t = rel_vectors.transpose(0, 2, 1)
     smem = pl.BlockSpec(memory_space=pltpu.SMEM)
@@ -489,16 +533,22 @@
     edge_rows = pltpu.VMEM((edge_count, LANES), F32)
     padded = pltpu.VMEM((DIM, padded_rows), F32)
     message = pltpu.VMEM((slot_total * 4, LANES), F32)
-    state_two, grad_mixed, mixed_zero, slope_zero, sums = pl.pallas_call(
+    state_two, grad_mixed, mixed_zero, slope_zero, rel_one, sums, places = pl.pallas_call(
         forward_kernel,
-        out_shape=(half, half, wide, wide, jax.ShapeDtypeStruct((16, LANES), F32)),
+        out_shape=(
+            half,
+            half,
+            wide,
+            wide,
+            jax.ShapeDtypeStruct((edge_count, LANES), F32),
+            jax.ShapeDtypeStruct((16, LANES), F32),
+            jax.ShapeDtypeStruct((tiles, slot_total), jnp.int32),
+        ),
         in_specs=[anywhere] * 2 + [smem] * 3 + [vmem] * 5,
-        out_specs=(vmem,) * 5,
-        scratch_shapes=[
-            block,
-            block,
-            block,
-            block,
+        out_specs=(anywhere,) * 5 + (vmem,) * 2,
+        scratch_shapes=[block] * 6
+        + [
+            pltpu.VMEM((4 * rows, cols), BF16),
             pltpu.VMEM((2, 3, rows, cols), BF16),
             window,
             window,
@@ -511,7 +561,7 @@
             pltpu.VMEM((4, 256, 256), BF16),
             pltpu.VMEM((1, cols), jnp.int32),
             pltpu.VMEM((1, cols), F32),
-            pltpu.SemaphoreType.DMA((2,)),
+            pltpu.SemaphoreType.DMA((8 + 2 * CHUNKS,)),
             pltpu.SemaphoreType.DMA((2, 3, CHUNKS)),
             pltpu.SemaphoreType.DMA((2, 3, CHUNKS)),
         ],
@@ -525,12 +575,19 @@
     state_out, sums = pl.pallas_call(
         scatter_kernel,
         out_shape=(half, jax.ShapeDtypeStruct(packet, F32)),
-        in_specs=[anywhere, smem] + [vmem] * 7,
+        in_specs=[anywhere] * 4 + [smem] + [vmem] * 4,
         out_specs=(anywhere, vmem),
-        scratch_shapes=[window, window, edge_rows, padded, message, pltpu.SemaphoreType.DMA],
+        scratch_shapes=[pltpu.VMEM((rows * 16, LANES), F32)] * SUMS
+        + [
+            edge_rows,
+            pltpu.VMEM((4 * rows, cols), BF16),
+            pltpu.VMEM((4 * rows, cols), BF16),
+            message,
+            pltpu.SemaphoreType.DMA((4,)),
+        ],
         compiler_params=pltpu.CompilerParams(vmem_limit_bytes=VMEM_BYTES),
         name="scatter_terms",
-    )(state_two, slots, edges, grad_mixed, rel_t, mixed_zero, slope_zero, cotangent, sums)
+    )(state_two, mixed_zero, slope_zero, rel_one, in_memory_order(places), edges, grad_mixed, cotangent, sums)
     weight_grads, bias_grads = pl.pallas_call(
         total_kernel,
         out_shape=(jax.ShapeDtypeStruct((2, DIM, DIM), F32), jax.ShapeDtypeStruct((2, DIM), F32)),

time: 179 us -> 165 us (0.922)
  Pallas kernels: 176 us -> 162 us
    pallas_call x1, Pallas kernels: 112 us -> 104 us  [body(): pl.pallas_call(forward_kernel, out_shape=(half, half, wide, wide, jax.Sha...]
    pallas_call x1, Pallas kernels: 48.5 us -> 43.3 us  [body(): pl.pallas_call(scatter_kernel, out_shape=(half, jax.ShapeDtypeStruct(pack...]
where the time goes in v4:
time: 165 us
  Pallas kernels  162 us (98%)
  local copies, waits for them, and re-layouts  2.57 us (2%)
    pallas_call x1, Pallas kernels, body(): pl.pallas_call(forward_kernel, out_shape=(half, half, wide, wide, jax.Sha...  104 us
    pallas_call x1, Pallas kernels, body(): pl.pallas_call(scatter_kernel, out_shape=(half, jax.ShapeDtypeStruct(pack...  43.3 us
    pallas_call x1, Pallas kernels, body(): pl.pallas_call(total_kernel, out_shape=(jax.ShapeDtypeStruct((2, DIM, DIM...  14.3 us

profile of v4, /device:TPU:0, one launch (start us, length us, event | category | flops | bytes accessed | tf_op | source)
XLA Modules:
  0.0 165.0 jit_solution(7262318580669720744)
XLA Ops:
  0.6 104.1 %two_layers.1 = (bf16[1024,512]{1,0:T(8,128)(2,1)}, bf16[1024,512]{1,0:T(8,128)(2,1)}, bf16[4096,512]{1,0:T(8,128)(2,1)}, bf16[4096,512]{1,0:T(8,128)(2,1)}, f32...) custom-call(bf16[1024,512]{1,0:T(8,128)(2,1)} %state_hbm.1, bf16[1024,512]{1,0:T(8,128)(2,1)} %cot_ref.1, ...), custom_call_target="tpu_custom_call" | custom-call | tf_op jit(solution)/shard_map/two_layers/pallas_call | solution.py:536
  104.7 43.3 %scatter_terms.1 = (bf16[1024,512]{1,0:T(8,128)(2,1)}, f32[24,128]{1,0:T(8,128)}) custom-call(bf16[1024,512]{1,0:T(8,128)(2,1)} %get-tuple-element.14.state_in, bf16[4096,512]{1,0:T(8,128)(2,1)} %get-tuple-element.15.mixed_in, bf16[4096,512]{1,0:T(8,128)(2,1)} %get-tuple-element.16.slope_in, f32[8192,128]{1,0:T(8,128)} %get-tuple-element.17.rel_in, ...), custom_call_target="tpu_custom_call" | custom-call | tf_op jit(solution)/shard_map/scatter_terms/pallas_call | solution.py:575
  148.0 14.3 %total_sums.1 = (f32[2,32,32]{2,1,0:T(8,128)}, f32[2,32]{1,0:T(2,128)}) custom-call(f32[24,128]{1,0:T(8,128)} %get-tuple-element.22.sums_ref), custom_call_target="tpu_custom_call" | custom-call | tf_op jit(solution)/shard_map/total_sums/pallas_call | solution.py:591
  162.4 1.4 copy.14
  163.8 1.2 copy.15

commit v5 on v4

--- a/solution.py
+++ b/solution.py
@@ -1,3 +1,5 @@
+import functools
+
 import jax
 import jax.numpy as jnp
 from jax import lax
@@ -13,6 +15,7 @@
 RING = 16
 WINDOW = 3
 SUMS = 4
+COLLECT = 512
 F32 = jnp.float32
 BF16 = jnp.bfloat16
 MESH = pl.DeviceIdType.MESH
@@ -74,23 +77,18 @@
         target[:, whole : whole + LANES] = jnp.concatenate([columns_ref[:, whole:count], rest], axis=1)
 
 
-def relation_rows(target, table_ref, edges_v):
-    parts = table_ref.shape[1] // LANES
-    tiles, slot_total = edges_v.shape[1:]
-
-    def tile_step(tile):
-        row = edges_v[2, pl.ds(tile, 1), :]
-        for q in range(slot_total // LANES):
-            ids = jnp.broadcast_to(row[:, q * LANES : (q + 1) * LANES], (DIM, LANES))
-            lane, part = lax.rem(ids, LANES), ids // LANES
-            found = jnp.zeros((DIM, LANES), F32)
-            for j in range(parts):
-                columns = table_ref[:, j * LANES : (j + 1) * LANES]
-                found = jnp.where(part == j, jnp.take_along_axis(columns, lane, axis=1), found)
-            at = pl.multiple_of(tile * slot_total + q * LANES, LANES)
-            target[pl.ds(at, LANES), :] = jnp.concatenate([found] * 4, axis=0).T
-
-    each(tiles, tile_step)
+def relation_rows(target, table_ref, edges_v, tile):
+    slot_total = edges_v.shape[2]
+    row = edges_v[2, pl.ds(tile, 1), :]
+    for q in range(slot_total // LANES):
+        ids = jnp.broadcast_to(row[:, q * LANES : (q + 1) * LANES], (DIM, LANES))
+        lane, part = ids & (LANES - 1), ids >> 7
+        found = jnp.zeros((DIM, LANES), F32)
+        for j in range(table_ref.shape[1] // LANES):
+            columns = table_ref[:, j * LANES : (j + 1) * LANES]
+            found = jnp.where(part == j, jnp.take_along_axis(columns, lane, axis=1), found)
+        at = pl.multiple_of(tile * slot_total + q * LANES, LANES)
+        target[pl.ds(at, LANES), :] = jnp.concatenate([found] * 4, axis=0).T
 
 
 def block_diagonal(matrix):
@@ -232,11 +230,8 @@
     each(CHUNKS, start_first)
 
     spread_table(table_ref, table_t)
-    for layer, target in enumerate((rel_a, rel_b)):
-        pad_columns(padded, rel_t.at[layer])
-        relation_rows(target, padded, edges_v)
-    rel_copy = pltpu.make_async_copy(rel_b, rel_out, copy_sem.at[2])
-    rel_copy.start()
+    for layer in range(2):
+        pad_columns(padded.at[layer], rel_t.at[layer])
     places_out[...] = edges_v[0] * 4
     lane = lax.broadcasted_iota(jnp.int32, (1, LANES), 1) // DIM
     for c in range(4):
@@ -258,7 +253,13 @@
     own_copy.wait()
     each(CHUNKS, lambda k: fill(win_a, 1, k, own[chunk_rows(k), :]))
 
+    def relations_of(layer, target, k):
+        relation_rows(target, padded.at[layer], edges_v, 2 * k)
+        relation_rows(target, padded.at[layer], edges_v, 2 * k + 1)
+
     def take_first_mirror(k):
+        relations_of(0, rel_a, k)
+        relations_of(1, rel_b, k)
         relay_chunk(0, k)
 
         @pl.when(jnp.logical_and(at_end, k + WINDOW < CHUNKS))
@@ -273,6 +274,8 @@
             fill(win_a, quarter, k, inbox[0, way, chunk_rows(k), :])
 
     each(CHUNKS, take_first_mirror)
+    rel_copy = pltpu.make_async_copy(rel_b, rel_out, copy_sem.at[2])
+    rel_copy.start()
     each(CHUNKS, take_first_sides)
 
     def next_state(state, update, quarter, k, half):
@@ -313,16 +316,16 @@
             cols = slice(half * 256, half * 256 + 256)
             update = split_dot(mixed_ref[:, cols], wide_ref[0], wide_ref[1]) + bias_zero
             middle[at, cols] = next_state(own[at, cols], update, 1, k, half)
-        @pl.when(k >= 3)
-        def _():
-            take_second_mirror(k - 3)
+        @pl.when(k >= 2)
+        def _():
+            take_second_mirror(k - 2)
 
         @pl.when(k >= 5)
         def _():
             take_second_sides(k - 5)
 
     each(CHUNKS, zero_step)
-    each(3, lambda k: take_second_mirror(k + CHUNKS - 3))
+    each(2, lambda k: take_second_mirror(k + CHUNKS - 2))
     each(5, lambda k: take_second_sides(k + CHUNKS - 5))
     cot_copy.wait()
     window_copies = [pltpu.make_async_copy(slope_ref, slope_out, copy_sem.at[3])]
@@ -375,17 +378,22 @@
 
 
 def scatter_kernel(
-    state_in, mixed_in, slope_in, rel_in, places_s, edges_v, grad_ref, cot_ref, sums_in, state_out, sums_out,
-    first_ref, second_ref, third_ref, fourth_ref, rel_ref, mixed_ref, slope_ref, term_ref, copy_sem,
+    state_in, mixed_in, slope_in, rel_in, cot_in, places_s, edges_v, grad_ref, sums_in, state_out, sums_out,
+    first_ref, second_ref, third_ref, fourth_ref, rel_ref, mixed_ref, slope_ref, cot_ref, state_ref, term_ref, copy_sem,
 ):
     copies = [
         pltpu.make_async_copy(source, target, copy_sem.at[i])
         for i, (source, target) in enumerate(
-            ((rel_in, rel_ref), (state_in, state_out), (mixed_in, mixed_ref), (slope_in, slope_ref))
+            ((state_in, state_ref), (mixed_in, mixed_ref), (slope_in, slope_ref), (cot_in, cot_ref))
         )
     ]
-    for copy in copies:
-        copy.start()
+    part_rows = rel_ref.shape[0] // 4
+
+    def rel_part(i):
+        at = pl.ds(pl.multiple_of(i * part_rows, part_rows), part_rows)
+        return pltpu.make_async_copy(rel_in.at[at, :], rel_ref.at[at, :], copy_sem.at[5 + i])
+
+    rel_part(0).start()
     totals = (first_ref, second_ref, third_ref, fourth_ref)
     tiles, slot_total = edges_v.shape[1:]
     half_total = slot_total // 2
@@ -396,7 +404,12 @@
             total[at, :] = jnp.zeros((256, LANES), F32)
 
     each(first_ref.shape[0] // 256, clear)
-    copies[0].wait()
+    rel_part(0).wait()
+    for i in range(1, 4):
+        rel_part(i).start()
+    for copy in copies:
+        copy.start()
+    state_copy = pltpu.make_async_copy(state_ref, state_out, copy_sem.at[4])
 
     def make_terms(tile, half):
         edges = slice(half * half_total, half * half_total + half_total)
@@ -418,38 +431,50 @@
     make_terms(0, 0)
 
     def tile_step(tile):
+        @pl.when(jnp.logical_and(tile & 3 == 3, tile < tiles - 1))
+        def _():
+            rel_part(tile // 4 + 1).wait()
+
         add_terms(tile, 0)
         make_terms(tile, 1)
         add_terms(tile, 1)
         make_terms(jnp.minimum(tile + 1, tiles - 1), 0)
 
     each(tiles, tile_step)
-    for copy in copies[1:]:
+    for copy in copies:
         copy.wait()
-
-    def collect(i, carry):
+    state_copy.start()
+
+    rows = cot_ref.shape[0]
+
+    def collect(quarter, i, carry):
         product, bias_sum = carry
-        start = pl.multiple_of(i * CHUNK, CHUNK)
-        at = pl.ds(start, CHUNK)
-        own_rows = pl.ds(pl.multiple_of(lax.rem(i, CHUNKS) * CHUNK, CHUNK), CHUNK)
-        mine = i // CHUNKS == 1
+        start = quarter * rows + pl.multiple_of(i * COLLECT, COLLECT)
+        at = pl.ds(start, COLLECT)
+        grads, mixed = [], []
         for c in range(4):
             cols = slice(c * LANES, (c + 1) * LANES)
-            place = pl.ds(start * 4 + c, CHUNK, stride=4)
+            place = pl.ds(start * 4 + c, COLLECT, stride=4)
             terms = (first_ref[place, :] + second_ref[place, :]) + (third_ref[place, :] + fourth_ref[place, :])
-            terms += jnp.where(mine, cot_ref[own_rows, cols].astype(F32), 0.0)
+            if quarter == 1:
+                own_rows = pl.ds(pl.multiple_of(i * COLLECT, COLLECT), COLLECT)
+                terms += cot_ref[own_rows, cols].astype(F32)
             grad = terms * slope_ref[at, cols].astype(F32)
-            product += product_of(mixed_ref[at, cols], grad.astype(BF16))
             bias_sum += jnp.sum(grad, axis=0, keepdims=True)
+            grads.append(grad.astype(BF16))
+            mixed.append(mixed_ref[at, cols])
+        product += product_of(jnp.concatenate(mixed, axis=0), jnp.concatenate(grads, axis=0))
         return product, bias_sum
 
-    product, bias_sum = lax.fori_loop(
-        0, 4 * CHUNKS, collect, (jnp.zeros((LANES, LANES), F32), jnp.zeros((1, LANES), F32))
-    )
+    sums = (jnp.zeros((LANES, LANES), F32), jnp.zeros((1, LANES), F32))
+    for quarter in range(4):
+        sums = lax.fori_loop(0, rows // COLLECT, functools.partial(collect, quarter), sums)
+    product, bias_sum = sums
     sums_out[0:8, :] = block_sums(product)
     sums_out[8:16, :] = sums_in[0:8, :]
     sub = lax.broadcasted_iota(jnp.int32, (8, LANES), 0)
     sums_out[16:24, :] = jnp.where(sub == 0, fold_lanes(jnp.broadcast_to(bias_sum, (8, LANES))), sums_in[8:16, :])
+    state_copy.wait()
 
 
 def total_kernel(
@@ -531,7 +556,7 @@
     block = pltpu.VMEM((rows, cols), BF16)
     window = pltpu.VMEM((rows * 4, 4, LANES), F32)
     edge_rows = pltpu.VMEM((edge_count, LANES), F32)
-    padded = pltpu.VMEM((DIM, padded_rows), F32)
+    padded = pltpu.VMEM((2, DIM, padded_rows), F32)
     message = pltpu.VMEM((slot_total * 4, LANES), F32)
     state_two, grad_mixed, mixed_zero, slope_zero, rel_one, sums, places = pl.pallas_call(
         forward_kernel,
@@ -575,19 +600,21 @@
     state_out, sums = pl.pallas_call(
         scatter_kernel,
         out_shape=(half, jax.ShapeDtypeStruct(packet, F32)),
-        in_specs=[anywhere] * 4 + [smem] + [vmem] * 4,
+        in_specs=[anywhere] * 5 + [smem] + [vmem] * 3,
         out_specs=(anywhere, vmem),
         scratch_shapes=[pltpu.VMEM((rows * 16, LANES), F32)] * SUMS
         + [
             edge_rows,
             pltpu.VMEM((4 * rows, cols), BF16),
             pltpu.VMEM((4 * rows, cols), BF16),
+            block,
+            block,
             message,
-            pltpu.SemaphoreType.DMA((4,)),
+            pltpu.SemaphoreType.DMA((9,)),
         ],
         compiler_params=pltpu.CompilerParams(vmem_limit_bytes=VMEM_BYTES),
         name="scatter_terms",
-    )(state_two, mixed_zero, slope_zero, rel_one, in_memory_order(places), edges, grad_mixed, cotangent, sums)
+    )(state_two, mixed_zero, slope_zero, rel_one, cotangent, in_memory_order(places), edges, grad_mixed, sums)
     weight_grads, bias_grads = pl.pallas_call(
         total_kernel,
         out_shape=(jax.ShapeDtypeStruct((2, DIM, DIM), F32), jax.ShapeDtypeStruct((2, DIM), F32)),

time: 165 us -> 137 us (0.83)
  Pallas kernels: 162 us -> 133 us
    pallas_call x1, Pallas kernels: 43.3 us -> 23.1 us  [body(): pl.pallas_call(scatter_kernel, out_shape=(half, jax.ShapeDtypeStruct(pack...]
    pallas_call x1, Pallas kernels: 104 us -> 95.6 us  [body(): pl.pallas_call(forward_kernel, out_shape=(half, half, wide, wide, jax.Sha...]
where the time goes in v5:
time: 137 us
  Pallas kernels  133 us (97%)
  local copies, waits for them, and re-layouts  2.57 us (2%)
    pallas_call x1, Pallas kernels, body(): pl.pallas_call(forward_kernel, out_shape=(half, half, wide, wide, jax.Sha...  95.6 us
    pallas_call x1, Pallas kernels, body(): pl.pallas_call(scatter_kernel, out_shape=(half, jax.ShapeDtypeStruct(pack...  23.1 us
    pallas_call x1, Pallas kernels, body(): pl.pallas_call(total_kernel, out_shape=(jax.ShapeDtypeStruct((2, DIM, DIM...  14.6 us

profile of v5, /device:TPU:0, one launch (start us, length us, event | category | flops | bytes accessed | tf_op | source)
XLA Modules:
  0.0 136.6 jit_solution(14836060739359162581)
XLA Ops:
  0.6 95.6 %two_layers.1 = (bf16[1024,512]{1,0:T(8,128)(2,1)}, bf16[1024,512]{1,0:T(8,128)(2,1)}, bf16[4096,512]{1,0:T(8,128)(2,1)}, bf16[4096,512]{1,0:T(8,128)(2,1)}, f32...) custom-call(bf16[1024,512]{1,0:T(8,128)(2,1)} %state_hbm.1, bf16[1024,512]{1,0:T(8,128)(2,1)} %cot_in.1, ...), custom_call_target="tpu_custom_call" | custom-call | tf_op jit(solution)/shard_map/two_layers/pallas_call | solution.py:561
  96.3 23.1 %scatter_terms.1 = (bf16[1024,512]{1,0:T(8,128)(2,1)}, f32[24,128]{1,0:T(8,128)}) custom-call(bf16[1024,512]{1,0:T(8,128)(2,1)} %get-tuple-element.14.state_in, bf16[4096,512]{1,0:T(8,128)(2,1)} %get-tuple-element.15.mixed_in, bf16[4096,512]{1,0:T(8,128)(2,1)} %get-tuple-element.16.slope_in, f32[8192,128]{1,0:T(8,128)} %get-tuple-element.17.rel_in, ...), custom_call_target="tpu_custom_call" | custom-call | tf_op jit(solution)/shard_map/scatter_terms/pallas_call | solution.py:600
  119.4 14.6 %total_sums.1 = (f32[2,32,32]{2,1,0:T(8,128)}, f32[2,32]{1,0:T(2,128)}) custom-call(f32[24,128]{1,0:T(8,128)} %get-tuple-element.22.sums_ref), custom_call_target="tpu_custom_call" | custom-call | tf_op jit(solution)/shard_map/total_sums/pallas_call | solution.py:618
  134.0 1.4 %copy.14 = f32[2,32,32]{2,1,0:T(8,128)} copy(f32[2,32,32]{2,1,0:T(8,128)} %get-tuple-element.29) | data formatting | bytes 16384
  135.4 1.2 copy.15

commit v6 on v5

--- a/solution.py
+++ b/solution.py
@@ -169,10 +169,10 @@
 
 
 def forward_kernel(
-    state_hbm, cot_hbm, slots_s, head_s, chosen_s, edges_v, table_t, rel_t, weight_ref, bias_ref,
+    state_hbm, cot_hbm, slots_hbm, edges_hbm, table_hbm, rel_hbm, head_s, chosen_s, weight_ref, bias_ref,
     state_out, grad_out, mixed_out, slope_out, rel_out, sums_out, places_out,
     own, middle, mixed_own, cot, state_ref, grad_ref, slope_ref, inbox, win_a, win_b, rel_a, rel_b, padded, table_ref,
-    message_ref, mixed_ref, wide_ref, head_ref, query_ref, copy_sem, send_sem, recv_sem,
+    message_ref, mixed_ref, wide_ref, head_ref, query_ref, slots_s, edges_v, table_t, rel_t, copy_sem, send_sem, recv_sem,
 ):
     node, position, targets = ring_targets()
     at_end = jnp.logical_or(position == 0, position == RING - 1)
@@ -180,10 +180,20 @@
     barrier = pltpu.get_barrier_semaphore()
     for target in targets:
         pl.semaphore_signal(barrier, inc=1, device_id={"node": target}, device_id_type=MESH)
+    first = 8 + 2 * CHUNKS
+    operand_copies = [
+        pltpu.make_async_copy(source, target, copy_sem.at[first + i])
+        for i, (source, target) in enumerate(
+            (
+                (table_hbm, table_t),
+                (rel_hbm, rel_t),
+                (edges_hbm, edges_v),
+                (slots_hbm.at[pl.ds(0, slots_s.shape[0])], slots_s),
+            )
+        )
+    ]
     own_copy = pltpu.make_async_copy(state_hbm, own, copy_sem.at[0])
     cot_copy = pltpu.make_async_copy(cot_hbm, cot, copy_sem.at[1])
-    own_copy.start()
-    cot_copy.start()
     pl.semaphore_wait(barrier, 3)
 
     def piece(trip, way, k, source):
@@ -228,6 +238,12 @@
             piece(0, 2, k, state_hbm).start()
 
     each(CHUNKS, start_first)
+    for copy in operand_copies:
+        copy.start()
+    own_copy.start()
+    cot_copy.start()
+    for copy in operand_copies:
+        copy.wait()
 
     spread_table(table_ref, table_t)
     for layer in range(2):
@@ -325,8 +341,11 @@
             take_second_sides(k - 5)
 
     each(CHUNKS, zero_step)
-    each(2, lambda k: take_second_mirror(k + CHUNKS - 2))
-    each(5, lambda k: take_second_sides(k + CHUNKS - 5))
+    take_second_sides(CHUNKS - 5)
+    take_second_mirror(CHUNKS - 2)
+    take_second_sides(CHUNKS - 4)
+    take_second_mirror(CHUNKS - 1)
+    each(3, lambda k: take_second_sides(k + CHUNKS - 3))
     cot_copy.wait()
     window_copies = [pltpu.make_async_copy(slope_ref, slope_out, copy_sem.at[3])]
     for quarter, source in enumerate((inbox.at[1, 0], mixed_own, inbox.at[1, 1], inbox.at[1, 2])):
@@ -378,8 +397,9 @@
 
 
 def scatter_kernel(
-    state_in, mixed_in, slope_in, rel_in, cot_in, places_s, edges_v, grad_ref, sums_in, state_out, sums_out,
-    first_ref, second_ref, third_ref, fourth_ref, rel_ref, mixed_ref, slope_ref, cot_ref, state_ref, term_ref, copy_sem,
+    state_in, mixed_in, slope_in, rel_in, cot_in, places_in, edges_in, grad_in, sums_in, state_out, sums_out,
+    first_ref, second_ref, third_ref, fourth_ref, rel_ref, mixed_ref, slope_ref, cot_ref, state_ref, term_ref,
+    places_s, edges_v, grad_ref, copy_sem,
 ):
     copies = [
         pltpu.make_async_copy(source, target, copy_sem.at[i])
@@ -393,6 +413,12 @@
         at = pl.ds(pl.multiple_of(i * part_rows, part_rows), part_rows)
         return pltpu.make_async_copy(rel_in.at[at, :], rel_ref.at[at, :], copy_sem.at[5 + i])
 
+    early = [
+        pltpu.make_async_copy(source, target, copy_sem.at[9 + i])
+        for i, (source, target) in enumerate(((places_in, places_s), (edges_in, edges_v), (grad_in, grad_ref)))
+    ]
+    for copy in early:
+        copy.start()
     rel_part(0).start()
     totals = (first_ref, second_ref, third_ref, fourth_ref)
     tiles, slot_total = edges_v.shape[1:]
@@ -404,6 +430,8 @@
             total[at, :] = jnp.zeros((256, LANES), F32)
 
     each(first_ref.shape[0] // 256, clear)
+    for copy in early:
+        copy.wait()
     rel_part(0).wait()
     for i in range(1, 4):
         rel_part(i).start()
@@ -478,7 +506,7 @@
 
 
 def total_kernel(
-    sums_ref, weight_out, bias_out, mine, first_buf, second_buf, first_send, first_recv, second_send, second_recv
+    sums_ref, total_out, mine, first_buf, second_buf, first_send, first_recv, second_send, second_recv
 ):
     node = lax.axis_index("node")
     query = lax.axis_index("query")
@@ -520,14 +548,19 @@
     total, finish_first = stage(sums_ref, first_buf, first_send, first_recv, in_first, first_peer, 8)
     mine[...] = total
     total, finish_second = stage(mine, second_buf, second_send, second_recv, position, second_peer, RING)
+    total_out[...] = total
+    finish_first()
+    finish_second()
+
+
+def unpack_kernel(total_ref, weight_out, bias_out):
+    total = total_ref[...]
     for l in range(2):
         packed = total[8 * l : 8 * l + 8, :]
         for k in range(4):
             moved = packed if k == 0 else pltpu.roll(packed, LANES - 32 * k, 1)
             weight_out[l, 8 * k : 8 * k + 8, :] = moved[:, 0:32]
     bias_out[...] = total[16:18, 0:32]
-    finish_first()
-    finish_second()
 
 
 def in_memory_order(table):
@@ -569,7 +602,7 @@
             jax.ShapeDtypeStruct((16, LANES), F32),
             jax.ShapeDtypeStruct((tiles, slot_total), jnp.int32),
         ),
-        in_specs=[anywhere] * 2 + [smem] * 3 + [vmem] * 5,
+        in_specs=[anywhere] * 6 + [smem] * 2 + [vmem] * 2,
         out_specs=(anywhere,) * 5 + (vmem,) * 2,
         scratch_shapes=[block] * 6
         + [
@@ -586,7 +619,11 @@
             pltpu.VMEM((4, 256, 256), BF16),
             pltpu.VMEM((1, cols), jnp.int32),
             pltpu.VMEM((1, cols), F32),
-            pltpu.SemaphoreType.DMA((8 + 2 * CHUNKS,)),
+            pltpu.SMEM((edge_count,), jnp.int32),
+            pltpu.VMEM(edges.shape, jnp.int32),
+            pltpu.VMEM(table_t.shape, F32),
+            pltpu.VMEM(rel_t.shape, F32),
+            pltpu.SemaphoreType.DMA((12 + 2 * CHUNKS,)),
             pltpu.SemaphoreType.DMA((2, 3, CHUNKS)),
             pltpu.SemaphoreType.DMA((2, 3, CHUNKS)),
         ],
@@ -595,12 +632,12 @@
         ),
         name="two_layers",
     )(
-        entity_state, cotangent, slots, query_head, query_relation, edges, table_t, rel_t, mix_weight, mix_bias
+        entity_state, cotangent, slots, edges, table_t, rel_t, query_head, query_relation, mix_weight, mix_bias
     )
     state_out, sums = pl.pallas_call(
         scatter_kernel,
         out_shape=(half, jax.ShapeDtypeStruct(packet, F32)),
-        in_specs=[anywhere] * 5 + [smem] + [vmem] * 3,
+        in_specs=[anywhere] * 8 + [vmem],
         out_specs=(anywhere, vmem),
         scratch_shapes=[pltpu.VMEM((rows * 16, LANES), F32)] * SUMS
         + [
@@ -610,16 +647,19 @@
             block,
             block,
             message,
-            pltpu.SemaphoreType.DMA((9,)),
+            pltpu.SMEM((edge_count,), jnp.int32),
+            pltpu.VMEM(edges.shape, jnp.int32),
+            block,
+            pltpu.SemaphoreType.DMA((12,)),
         ],
         compiler_params=pltpu.CompilerParams(vmem_limit_bytes=VMEM_BYTES),
         name="scatter_terms",
     )(state_two, mixed_zero, slope_zero, rel_one, cotangent, in_memory_order(places), edges, grad_mixed, sums)
-    weight_grads, bias_grads = pl.pallas_call(
+    total = pl.pallas_call(
         total_kernel,
-        out_shape=(jax.ShapeDtypeStruct((2, DIM, DIM), F32), jax.ShapeDtypeStruct((2, DIM), F32)),
+        out_shape=jax.ShapeDtypeStruct(packet, F32),
         in_specs=[vmem],
-        out_specs=(vmem,) * 2,
+        out_specs=vmem,
         scratch_shapes=[
             pltpu.VMEM(packet, F32),
             pltpu.VMEM((8,) + packet, F32),
@@ -632,6 +672,13 @@
         compiler_params=pltpu.CompilerParams(collective_id=1, has_side_effects=True),
         name="total_sums",
     )(sums)
+    weight_grads, bias_grads = pl.pallas_call(
+        unpack_kernel,
+        out_shape=(jax.ShapeDtypeStruct((2, DIM, DIM), F32), jax.ShapeDtypeStruct((2, DIM), F32)),
+        in_specs=[vmem],
+        out_specs=(vmem,) * 2,
+        name="unpack_sums",
+    )(total)
     return state_out, weight_grads, bias_grads
 
 

time: 137 us -> 133 us (0.971)
  local copies, waits for them, and re-layouts: 2.57 us -> 0 us
    unnamed x2 -> x0, local copies, waits for them, and re-layouts: 2.57 us -> none
    pallas_call x1, Pallas kernels: 95.6 us -> 94 us  [body(): pl.pallas_call(forward_kernel, out_shape=(half, half, wide, wide, jax.Sha...]
    pallas_call x1 -> x2, Pallas kernels: 14.6 us -> 15.9 us  [the longest x1 14.5 us: body(): pl.pallas_call(total_kernel, out_shape=jax.ShapeDtypeStruct(packet, F32),...]
where the time goes in v6:
time: 133 us
  Pallas kernels  132 us (99%)
    pallas_call x1, Pallas kernels, body(): pl.pallas_call(forward_kernel, out_shape=(half, half, wide, wide, jax.Sha...  94 us
    pallas_call x1, Pallas kernels, body(): pl.pallas_call(scatter_kernel, out_shape=(half, jax.ShapeDtypeStruct(pack...  22.6 us
    pallas_call x1, Pallas kernels, body(): pl.pallas_call(total_kernel, out_shape=jax.ShapeDtypeStruct(packet, F32),...  14.5 us

profile of v6, /device:TPU:0, one launch (start us, length us, event | category | flops | bytes accessed | tf_op | source)
XLA Modules:
  0.0 133.1 jit_solution(4310881867699515304)
XLA Ops:
  0.6 94.0 %two_layers.1 = (bf16[1024,512]{1,0:T(8,128)(2,1)}, bf16[1024,512]{1,0:T(8,128)(2,1)}, bf16[4096,512]{1,0:T(8,128)(2,1)}, bf16[4096,512]{1,0:T(8,128)(2,1)}, f32...) custom-call(bf16[1024,512]{1,0:T(8,128)(2,1)} %state_hbm.1, bf16[1024,512]{1,0:T(8,128)(2,1)} %cot_in.1, ...), custom_call_target="tpu_custom_call" | custom-call | tf_op jit(solution)/shard_map/two_layers/pallas_call | solution.py:594
  94.6 22.6 %scatter_terms.1 = (bf16[1024,512]{1,0:T(8,128)(2,1)}, f32[24,128]{1,0:T(8,128)}) custom-call(bf16[1024,512]{1,0:T(8,128)(2,1)} %get-tuple-element.14.state_in, bf16[4096,512]{1,0:T(8,128)(2,1)} %get-tuple-element.15.mixed_in, bf16[4096,512]{1,0:T(8,128)(2,1)} %get-tuple-element.16.slope_in, f32[8192,128]{1,0:T(8,128)} %get-tuple-element.17.rel_in, ...), custom_call_target="tpu_custom_call" | custom-call | tf_op jit(solution)/shard_map/scatter_terms/pallas_call | solution.py:637
  117.2 14.5 %total_sums.1.total_ref = f32[24,128]{1,0:T(8,128)} custom-call(f32[24,128]{1,0:T(8,128)} %get-tuple-element.22.sums_ref), custom_call_target="tpu_custom_call" | custom-call | tf_op jit(solution)/shard_map/total_sums/pallas_call | solution.py:658
  131.8 1.4 %unpack_sums.1 = (f32[2,32,32]{2,1,0:T(8,128)}, f32[2,32]{1,0:T(2,128)}) custom-call(f32[24,128]{1,0:T(8,128)} %total_sums.1.total_ref), custom_call_target="tpu_custom_call" | custom-call | tf_op jit(solution)/shard_map/unpack_sums/pallas_call | solution.py:675

commit v7 on v6

--- a/solution.py
+++ b/solution.py
@@ -146,18 +146,20 @@
 def sum_chunk(k, first_row, slots_s, edges_v, head_ref, query_ref, win_ref, rel_ref, message_ref, mixed_ref):
     slot_total = edges_v.shape[2]
 
+    def gather(j):
+        base = slot_base(2 * k + j)
+        for edge in range(slot_total):
+            message_ref[j, 4 * edge : 4 * edge + 4, :] = win_ref[slots_s[base + slot_step(edge)]]
+
     def tile_step(j):
         tile = 2 * k + j
 
-        base = slot_base(tile)
-        for edge in range(slot_total):
-            message_ref[4 * edge : 4 * edge + 4, :] = win_ref[slots_s[base + slot_step(edge)]]
         onehot = target_onehot(edges_v, tile)
-        row = pl.multiple_of(j * TILE, TILE)
+        row = j * TILE
         ids = first_row + tile * TILE + lax.broadcasted_iota(jnp.int32, (TILE, LANES), 0)
         scale = rel_ref[pl.ds(pl.multiple_of(tile * slot_total, slot_total), slot_total), :]
         message = jnp.concatenate(
-            [(message_ref[pl.ds(c, slot_total, stride=4), :] * scale).astype(BF16) for c in range(4)], axis=1
+            [(message_ref[j, pl.ds(c, slot_total, stride=4), :] * scale).astype(BF16) for c in range(4)], axis=1
         )
         summed = jnp.dot(onehot, message, preferred_element_type=F32)
         for c in range(4):
@@ -165,7 +167,10 @@
             start = jnp.where(ids == head_ref[:, cols], query_ref[:, cols], 0.0)
             mixed_ref[pl.ds(row, TILE), cols] = start + summed[:, cols]
 
-    each(2, tile_step)
+    for j in range(2):
+        gather(j)
+    for j in range(2):
+        tile_step(j)
 
 
 def forward_kernel(
@@ -614,7 +619,7 @@
             edge_rows,
             padded,
             pltpu.VMEM((rel_rows, 4, LANES), F32),
-            message,
+            pltpu.VMEM((2, slot_total * 4, LANES), F32),
             pltpu.VMEM((CHUNK, cols), F32),
             pltpu.VMEM((4, 256, 256), BF16),
             pltpu.VMEM((1, cols), jnp.int32),

time: 133 us -> 131 us (0.985)
  Pallas kernels: 132 us -> 130 us
    pallas_call x1, Pallas kernels: 94 us -> 91.8 us  [body(): pl.pallas_call(forward_kernel, out_shape=(half, half, wide, wide, jax.Sha...]
where the time goes in v7:
time: 131 us
  Pallas kernels  130 us (99%)
    pallas_call x1, Pallas kernels, body(): pl.pallas_call(forward_kernel, out_shape=(half, half, wide, wide, jax.Sha...  91.8 us
    pallas_call x1, Pallas kernels, body(): pl.pallas_call(scatter_kernel, out_shape=(half, jax.ShapeDtypeStruct(pack...  22.6 us
    pallas_call x1, Pallas kernels, body(): pl.pallas_call(total_kernel, out_shape=jax.ShapeDtypeStruct(packet, F32),...  14.3 us

profile of v7, /device:TPU:0, one launch (start us, length us, event | category | flops | bytes accessed | tf_op | source)
XLA Modules:
  0.0 130.8 jit_solution(9633541711917367652)
XLA Ops:
  0.6 91.8 %two_layers.1 = (bf16[1024,512]{1,0:T(8,128)(2,1)}, bf16[1024,512]{1,0:T(8,128)(2,1)}, bf16[4096,512]{1,0:T(8,128)(2,1)}, bf16[4096,512]{1,0:T(8,128)(2,1)}, f32...) custom-call(bf16[1024,512]{1,0:T(8,128)(2,1)} %state_hbm.1, bf16[1024,512]{1,0:T(8,128)(2,1)} %cot_in.1, ...), custom_call_target="tpu_custom_call" | custom-call | tf_op jit(solution)/shard_map/two_layers/pallas_call | solution.py:599
  92.5 22.6 %scatter_terms.1 = (bf16[1024,512]{1,0:T(8,128)(2,1)}, f32[24,128]{1,0:T(8,128)}) custom-call(bf16[1024,512]{1,0:T(8,128)(2,1)} %get-tuple-element.14.state_in, bf16[4096,512]{1,0:T(8,128)(2,1)} %get-tuple-element.15.mixed_in, bf16[4096,512]{1,0:T(8,128)(2,1)} %get-tuple-element.16.slope_in, f32[8192,128]{1,0:T(8,128)} %get-tuple-element.17.rel_in, ...), custom_call_target="tpu_custom_call" | custom-call | tf_op jit(solution)/shard_map/scatter_terms/pallas_call | solution.py:642
  115.1 14.3 %total_sums.1.total_ref = f32[24,128]{1,0:T(8,128)} custom-call(f32[24,128]{1,0:T(8,128)} %get-tuple-element.22.sums_ref), custom_call_target="tpu_custom_call" | custom-call | tf_op jit(solution)/shard_map/total_sums/pallas_call | solution.py:663
  129.4 1.4 %unpack_sums.1 = (f32[2,32,32]{2,1,0:T(8,128)}, f32[2,32]{1,0:T(2,128)}) custom-call(f32[24,128]{1,0:T(8,128)} %total_sums.1.total_ref), custom_call_target="tpu_custom_call" | custom-call | tf_op jit(solution)/shard_map/unpack_sums/pallas_call | solution.py:680

commit v8 on v7

--- a/solution.py
+++ b/solution.py
@@ -14,8 +14,10 @@
 CHUNKS = 8
 RING = 16
 WINDOW = 3
+PIECE = 64
+PIECES = CHUNK // PIECE
 SUMS = 4
-COLLECT = 512
+COLLECT = 1024
 F32 = jnp.float32
 BF16 = jnp.bfloat16
 MESH = pl.DeviceIdType.MESH
@@ -201,36 +203,47 @@
     cot_copy = pltpu.make_async_copy(cot_hbm, cot, copy_sem.at[1])
     pl.semaphore_wait(barrier, 3)
 
-    def piece(trip, way, k, source):
+    def piece(trip, way, i, source):
+        at = pl.ds(pl.multiple_of(i * PIECE, PIECE), PIECE)
         return pltpu.make_async_remote_copy(
-            src_ref=source.at[chunk_rows(k), :],
-            dst_ref=inbox.at[trip, way, chunk_rows(k), :],
-            send_sem=send_sem.at[trip, way, k],
-            recv_sem=recv_sem.at[trip, way, k],
+            src_ref=source.at[at, :],
+            dst_ref=inbox.at[trip, way, at, :],
+            send_sem=send_sem.at[trip, way, i],
+            recv_sem=recv_sem.at[trip, way, i],
             device_id={"node": targets[way]},
             device_id_type=MESH,
         )
 
+    def start_chunk(trip, way, k, source):
+        for i in range(PIECES):
+            piece(trip, way, k * PIECES + i, source).start()
+
+    def receive_chunk(trip, way, k):
+        for i in range(PIECES):
+            piece(trip, way, k * PIECES + i, own).wait_recv()
+
     def send_sides(trip, k, source):
         @pl.when(position != RING - 1)
         def _():
-            piece(trip, 0, k, source).start()
+            start_chunk(trip, 0, k, source)
 
         @pl.when(position != 0)
         def _():
-            piece(trip, 1, k, source).start()
+            start_chunk(trip, 1, k, source)
 
     def relay_chunk(trip, k):
         mirrored = inbox.at[trip, 2]
-        piece(trip, 2, k, mirrored).wait_recv()
-
-        @pl.when(position == RING - 1)
-        def _():
-            piece(trip, 0, k, mirrored).start()
-
-        @pl.when(position == 0)
-        def _():
-            piece(trip, 1, k, mirrored).start()
+        for i in range(PIECES):
+            j = k * PIECES + i
+            piece(trip, 2, j, mirrored).wait_recv()
+
+            @pl.when(position == RING - 1)
+            def _():
+                piece(trip, 0, j, mirrored).start()
+
+            @pl.when(position == 0)
+            def _():
+                piece(trip, 1, j, mirrored).start()
 
     def fill(win, quarter, k, block):
         spread_rows(win, quarter * rows + k * CHUNK, block.astype(F32))
@@ -240,7 +253,7 @@
 
         @pl.when(jnp.logical_or(jnp.logical_not(at_end), k < WINDOW))
         def _():
-            piece(0, 2, k, state_hbm).start()
+            start_chunk(0, 2, k, state_hbm)
 
     each(CHUNKS, start_first)
     for copy in operand_copies:
@@ -285,13 +298,13 @@
 
         @pl.when(jnp.logical_and(at_end, k + WINDOW < CHUNKS))
         def _():
-            piece(0, 2, k + WINDOW, state_hbm).start()
+            start_chunk(0, 2, k + WINDOW, state_hbm)
 
         fill(win_a, 3, k, inbox[0, 2, chunk_rows(k), :])
 
     def take_first_sides(k):
         for way, quarter in ((0, 0), (1, 2)):
-            piece(0, way, k, own).wait_recv()
+            receive_chunk(0, way, k)
             fill(win_a, quarter, k, inbox[0, way, chunk_rows(k), :])
 
     each(CHUNKS, take_first_mirror)
@@ -324,14 +337,14 @@
 
     def take_second_sides(k):
         for way, quarter in ((0, 0), (1, 2)):
-            piece(1, way, k, own).wait_recv()
+            receive_chunk(1, way, k)
             remote_state(way, quarter, k)
 
     def zero_step(k):
         sum_chunk(k, first_row, slots_s, edges_v, head_ref, query_ref, win_a, rel_a, message_ref, mixed_ref)
         at = chunk_rows(k)
         mixed_own[at, :] = mixed_ref[...].astype(BF16)
-        piece(1, 2, k, mixed_own).start()
+        start_chunk(1, 2, k, mixed_own)
         send_sides(1, k, mixed_own)
         for half in range(2):
             cols = slice(half * 256, half * 256 + 256)
@@ -378,10 +391,12 @@
             sigma = jax.nn.sigmoid(update)
             state_ref[at, cols] = (middle[at, cols].astype(F32) + update * sigma).astype(BF16)
             grad = cot[at, cols].astype(F32) * (sigma * (1.0 + update * (1.0 - sigma)))
-            grad_ref[at, cols] = split_dot(grad, wide_ref[2], wide_ref[3], 1).astype(BF16)
+            rounded = grad.astype(BF16)
+            back = half_dot(rounded, wide_ref[2], 1) + half_dot(rounded, wide_ref[3], 1)
+            grad_ref[at, cols] = back.astype(BF16)
             for c in range(2):
                 part = slice(c * LANES, (c + 1) * LANES)
-                product += product_of(mixed[:, part].astype(BF16), grad[:, part].astype(BF16))
+                product += product_of(mixed[:, part].astype(BF16), rounded[:, part])
                 bias_sum += jnp.sum(grad[:, part], axis=0, keepdims=True)
         for copy in result_copies(k):
             copy.start()
@@ -394,7 +409,7 @@
     sums_out[8:16, :] = fold_lanes(jnp.broadcast_to(bias_sum, (8, LANES)))
     for trip in range(2):
         for way in range(3):
-            each(CHUNKS, lambda k: piece(trip, way, k, own).wait_send())
+            each(CHUNKS * PIECES, lambda i: piece(trip, way, i, own).wait_send())
     rel_copy.wait()
     for copy in window_copies:
         copy.wait()
@@ -629,8 +644,8 @@
             pltpu.VMEM(table_t.shape, F32),
             pltpu.VMEM(rel_t.shape, F32),
             pltpu.SemaphoreType.DMA((12 + 2 * CHUNKS,)),
-            pltpu.SemaphoreType.DMA((2, 3, CHUNKS)),
-            pltpu.SemaphoreType.DMA((2, 3, CHUNKS)),
+            pltpu.SemaphoreType.DMA((2, 3, CHUNKS * PIECES)),
+            pltpu.SemaphoreType.DMA((2, 3, CHUNKS * PIECES)),
         ],
         compiler_params=pltpu.CompilerParams(
             vmem_limit_bytes=VMEM_BYTES, collective_id=0, has_side_effects=True

time: 131 us -> 130 us (level)
    pallas_call x1, Pallas kernels: 91.8 us -> 90.5 us  [body(): pl.pallas_call(forward_kernel, out_shape=(half, half, wide, wide, jax.Sha...]
where the time goes in v8:
time: 130 us; the launch traced here: 129 us
  Pallas kernels  129 us (99%)
    pallas_call x1, Pallas kernels, body(): pl.pallas_call(forward_kernel, out_shape=(half, half, wide, wide, jax.Sha...  90.5 us
    pallas_call x1, Pallas kernels, body(): pl.pallas_call(scatter_kernel, out_shape=(half, jax.ShapeDtypeStruct(pack...  22 us
    pallas_call x1, Pallas kernels, body(): pl.pallas_call(total_kernel, out_shape=jax.ShapeDtypeStruct(packet, F32),...  14.9 us

profile of v8, /device:TPU:0, one launch (start us, length us, event | category | flops | bytes accessed | tf_op | source)
XLA Modules:
  0.0 129.4 jit_solution(16357264295834673563)
XLA Ops:
  0.6 90.5 %two_layers.1 = (bf16[1024,512]{1,0:T(8,128)(2,1)}, bf16[1024,512]{1,0:T(8,128)(2,1)}, bf16[4096,512]{1,0:T(8,128)(2,1)}, bf16[4096,512]{1,0:T(8,128)(2,1)}, f32...) custom-call(bf16[1024,512]{1,0:T(8,128)(2,1)} %state_hbm.1, bf16[1024,512]{1,0:T(8,128)(2,1)} %cot_in.1, ...), custom_call_target="tpu_custom_call" | custom-call | tf_op jit(solution)/shard_map/two_layers/pallas_call | solution.py:614
  91.2 22.0 %scatter_terms.1 = (bf16[1024,512]{1,0:T(8,128)(2,1)}, f32[24,128]{1,0:T(8,128)}) custom-call(bf16[1024,512]{1,0:T(8,128)(2,1)} %get-tuple-element.14.state_in, bf16[4096,512]{1,0:T(8,128)(2,1)} %get-tuple-element.15.mixed_in, bf16[4096,512]{1,0:T(8,128)(2,1)} %get-tuple-element.16.slope_in, f32[8192,128]{1,0:T(8,128)} %get-tuple-element.17.rel_in, ...), custom_call_target="tpu_custom_call" | custom-call | tf_op jit(solution)/shard_map/scatter_terms/pallas_call | solution.py:657
  113.1 14.9 %total_sums.1.total_ref = f32[24,128]{1,0:T(8,128)} custom-call(f32[24,128]{1,0:T(8,128)} %get-tuple-element.22.sums_ref), custom_call_target="tpu_custom_call" | custom-call | tf_op jit(solution)/shard_map/total_sums/pallas_call | solution.py:678
  128.0 1.4 %unpack_sums.1 = (f32[2,32,32]{2,1,0:T(8,128)}, f32[2,32]{1,0:T(2,128)}) custom-call(f32[24,128]{1,0:T(8,128)} %total_sums.1.total_ref), custom_call_target="tpu_custom_call" | custom-call | tf_op jit(solution)/shard_map/unpack_sums/pallas_call | solution.py:695
